TPU v7x, 256 devices: a whole 4x4x8 slice. The times are simulated.
256 devices in a mesh: chan: 32 (over z, x_lo, core), day: 8 (over x_hi, y).
Axes of the slice: x: 4 (x_hi: 2, x_lo: 2; x = x_hi * 2 + x_lo), y: 4, z: 8, core: 2. Of those that a mesh axis runs over, the one named last changes fastest.
Arguments:
- spectra: bfloat16 [8, 512, 2, 4096], P('day', 'chan'), may hold values from -6 to 6
- source_index: int32 [16], replicated, may hold values from 0 to 511, as said below
- interrogator: int32 [512], P('chan'), may hold values from 0 to 7, as said below
- lag_bounds: int32 [16, 2], replicated, may hold values from 0 to 256, as said below
Outputs:
- reference_stack: bfloat16 [16, 512, 256], P('day', 'chan')
- drift: float32 [8, 8], P('day')
Inputs may be any that keep to these rules, and one draw needn't show every extreme that they name: `source_index`: distinct channels. Each interrogator serves one contiguous run of channels, in rising order, of at least 32 channels. `lag_bounds`: first lag below end lag, and each window spans at least 128 lags.
All inputs are finite; a program needn't handle non-finite values.
Results may differ from a plain program's by a relative error of at most 0.0065.
Values may be sent and summed in bfloat16 or wider, within the bound.
No kernel may reach another device: no remote copies, remote signals or barrier semaphores. Data moves between devices by JAX's collectives and lax.ppermute only.
A program may use at most 64 MiB of HBM per device.

v0:
```python
import math

import jax
import jax.numpy as jnp
from jax import lax
from jax.sharding import PartitionSpec as P

LAGS = 256
NINT = 8


def from_root(value, axis, source):
    kept = jnp.where(lax.axis_index(axis) == source, value, 0).astype(value.dtype)
    return lax.psum(kept, axis)


def lag_table(bins, lags):
    freq = jnp.arange(bins, dtype=jnp.int32)
    shift = jnp.arange(lags, dtype=jnp.int32) - lags // 2
    phase = freq[:, None] * shift[None, :] % (2 * bins)
    angle = math.pi * phase.astype(jnp.float32) / bins
    scale = 1.0 / math.sqrt(bins)
    return jnp.concatenate([jnp.cos(angle) * scale, -jnp.sin(angle) * scale], 0).astype(
        jnp.bfloat16
    )


def per_device(spectra, source_index, interrogator, lag_bounds):
    day_dev, ch_dev, _, bins = spectra.shape
    nsrc = source_index.shape[0]
    lags = LAGS

    def fetch(source, buffer):
        chosen_chan = source_index[source]
        owner = chosen_chan // ch_dev
        local_row = chosen_chan - owner * ch_dev
        piece = lax.dynamic_slice_in_dim(spectra, local_row, 1, 1)
        arrived = from_root(piece, "chan", owner)
        return lax.dynamic_update_slice_in_dim(buffer, arrived, source, 1)

    sources = lax.fori_loop(0, nsrc, fetch, jnp.zeros((day_dev, nsrc, 2, bins), jnp.bfloat16))
    table = lag_table(bins, lags)
    block = math.gcd(nsrc, 16)

    def correlate_block(index, corr):
        chosen = sources[0].astype(jnp.float32)
        local = spectra[0].astype(jnp.float32)
        real_in = local[None, :, 0]
        imag_in = local[None, :, 1]
        real_src = chosen[:, None, 0]
        imag_src = chosen[:, None, 1]
        cross = jnp.concatenate(
            [real_in * real_src + imag_in * imag_src, imag_in * real_src - real_in * imag_src], -1
        )
        cross = cross.astype(jnp.bfloat16).reshape(block * ch_dev, 2 * bins)
        result = jnp.dot(cross, table, preferred_element_type=jnp.float32).reshape(
            1, block, ch_dev, lags
        )
        return result

    corr = lax.fori_loop(
        0, nsrc // block, correlate_block, jnp.zeros((day_dev, nsrc, ch_dev, lags), jnp.float32)
    )
    local_sum = jnp.sum(corr, 0)
    days = day_dev * lax.axis_size("day")
    total = lax.psum(local_sum, "day")
    ref_full = (total / days).astype(jnp.bfloat16)
    share = nsrc // lax.axis_size("day")
    ref_out = lax.dynamic_slice_in_dim(ref_full, lax.axis_index("day") * share, share, 0)
    ref_float = ref_full.astype(jnp.float32)
    lag_pos = jnp.arange(lags, dtype=jnp.int32)
    window = (
        (lag_pos[None, :] >= lag_bounds[:, 0:1]) & (lag_pos[None, :] < lag_bounds[:, 1:2])
    ).astype(jnp.float32)
    member = (interrogator[:, None] == jnp.arange(NINT, dtype=jnp.int32)[None, :]).astype(
        jnp.float32
    )
    day_corr = corr[0]
    padded = jnp.pad(day_corr, ((0, 0), (0, 0), (1, 1)))
    slope = 0.5 * (padded[:, :, 2:] - padded[:, :, :-2])
    weighted = window[:, None, :] * slope
    num_chan = jnp.sum(weighted * (day_corr - ref_float), axis=(0, 2))
    den_chan = jnp.sum(weighted * slope, axis=(0, 2))
    numers = [jnp.sum(num_chan[:, None] * member, 0)]
    denoms = [jnp.sum(den_chan[:, None] * member, 0)]
    numer, denom = lax.psum((jnp.stack(numers, 0), jnp.stack(denoms, 0)), "chan")
    drift = numer / (denom + 1e-06)
    return (ref_out, drift)


def solution(mesh):
    return jax.shard_map(
        per_device,
        mesh=mesh,
        in_specs=(P("day", "chan", None, None), P(), P("chan"), P()),
        out_specs=(P("day", "chan", None), P("day", None)),
        check_vma=False,
    )
```

profile of v0, /device:TPU:1, one launch (start us, length us, event | category | flops | bytes accessed | tf_op | source)
XLA Modules:
  0.0 1944.4 jit_solution(5148934047910936278)
XLA Ops:
  9.0 1759.0 %while.19 = (s32[]{:T(128)}, bf16[1,16,2,4096]{3,2,1,0:T(2,128)(2,1)S(1)}, s32[16]{0:T(128)}, bf16[1,16,2,4096]{3,2,1,0:T(2,128)(2,1)}, s32[]{:T(128)}, /*index=...) while((s32[]{:T(128)}, ...), condition=%wide.region_2.3_spmd, body=%wide.region_0.2_spmd.sunk | while | flops 16410 | bytes 98691 | solution.py:41
  14.2 107.7 %psum.39 = bf16[1,1,2,4096]{3,2,1,0:T(2,128)(2,1)S(1)} all-reduce(bf16[1,1,2,4096]{3,2,1,0:T(2,128)(2,1)S(1)} %broadcast_select_fusion.2), channel_id=1, replica_groups=mesh['chan'=32,'day'=8] {'chan'}, use_global_device_ids=true, to_apply=%region_1.1 | all-reduce | flops 8192 | bytes 32768 | tf_op jit(solution)/shard_map/while/body/eval_jaxpr/psum | solution.py:14
  127.2 104.5 %psum.39 = bf16[1,1,2,4096]{3,2,1,0:T(2,128)(2,1)S(1)} all-reduce(bf16[1,1,2,4096]{3,2,1,0:T(2,128)(2,1)S(1)} %broadcast_select_fusion.2), channel_id=1, replica_groups=mesh['chan'=32,'day'=8] {'chan'}, use_global_device_ids=true, to_apply=%region_1.1 | all-reduce | flops 8192 | bytes 32768 | tf_op jit(solution)/shard_map/while/body/eval_jaxpr/psum | solution.py:14
  236.9 104.5 %psum.39 = bf16[1,1,2,4096]{3,2,1,0:T(2,128)(2,1)S(1)} all-reduce(bf16[1,1,2,4096]{3,2,1,0:T(2,128)(2,1)S(1)} %broadcast_select_fusion.2), channel_id=1, replica_groups=mesh['chan'=32,'day'=8] {'chan'}, use_global_device_ids=true, to_apply=%region_1.1 | all-reduce | flops 8192 | bytes 32768 | tf_op jit(solution)/shard_map/while/body/eval_jaxpr/psum | solution.py:14
  341.4 1.2 dynamic_slice.29
  346.7 104.5 %psum.39 = bf16[1,1,2,4096]{3,2,1,0:T(2,128)(2,1)S(1)} all-reduce(bf16[1,1,2,4096]{3,2,1,0:T(2,128)(2,1)S(1)} %broadcast_select_fusion.2), channel_id=1, replica_groups=mesh['chan'=32,'day'=8] {'chan'}, use_global_device_ids=true, to_apply=%region_1.1 | all-reduce | flops 8192 | bytes 32768 | tf_op jit(solution)/shard_map/while/body/eval_jaxpr/psum | solution.py:14
  456.4 104.5 %psum.39 = bf16[1,1,2,4096]{3,2,1,0:T(2,128)(2,1)S(1)} all-reduce(bf16[1,1,2,4096]{3,2,1,0:T(2,128)(2,1)S(1)} %broadcast_select_fusion.2), channel_id=1, replica_groups=mesh['chan'=32,'day'=8] {'chan'}, use_global_device_ids=true, to_apply=%region_1.1 | all-reduce | flops 8192 | bytes 32768 | tf_op jit(solution)/shard_map/while/body/eval_jaxpr/psum | solution.py:14
  566.1 104.5 %psum.39 = bf16[1,1,2,4096]{3,2,1,0:T(2,128)(2,1)S(1)} all-reduce(bf16[1,1,2,4096]{3,2,1,0:T(2,128)(2,1)S(1)} %broadcast_select_fusion.2), channel_id=1, replica_groups=mesh['chan'=32,'day'=8] {'chan'}, use_global_device_ids=true, to_apply=%region_1.1 | all-reduce | flops 8192 | bytes 32768 | tf_op jit(solution)/shard_map/while/body/eval_jaxpr/psum | solution.py:14
  675.9 104.5 %psum.39 = bf16[1,1,2,4096]{3,2,1,0:T(2,128)(2,1)S(1)} all-reduce(bf16[1,1,2,4096]{3,2,1,0:T(2,128)(2,1)S(1)} %broadcast_select_fusion.2), channel_id=1, replica_groups=mesh['chan'=32,'day'=8] {'chan'}, use_global_device_ids=true, to_apply=%region_1.1 | all-reduce | flops 8192 | bytes 32768 | tf_op jit(solution)/shard_map/while/body/eval_jaxpr/psum | solution.py:14
  785.6 104.5 %psum.39 = bf16[1,1,2,4096]{3,2,1,0:T(2,128)(2,1)S(1)} all-reduce(bf16[1,1,2,4096]{3,2,1,0:T(2,128)(2,1)S(1)} %broadcast_select_fusion.2), channel_id=1, replica_groups=mesh['chan'=32,'day'=8] {'chan'}, use_global_device_ids=true, to_apply=%region_1.1 | all-reduce | flops 8192 | bytes 32768 | tf_op jit(solution)/shard_map/while/body/eval_jaxpr/psum | solution.py:14
  890.1 1.2 dynamic_slice.29
  895.3 104.5 %psum.39 = bf16[1,1,2,4096]{3,2,1,0:T(2,128)(2,1)S(1)} all-reduce(bf16[1,1,2,4096]{3,2,1,0:T(2,128)(2,1)S(1)} %broadcast_select_fusion.2), channel_id=1, replica_groups=mesh['chan'=32,'day'=8] {'chan'}, use_global_device_ids=true, to_apply=%region_1.1 | all-reduce | flops 8192 | bytes 32768 | tf_op jit(solution)/shard_map/while/body/eval_jaxpr/psum | solution.py:14
  1005.1 104.5 %psum.39 = bf16[1,1,2,4096]{3,2,1,0:T(2,128)(2,1)S(1)} all-reduce(bf16[1,1,2,4096]{3,2,1,0:T(2,128)(2,1)S(1)} %broadcast_select_fusion.2), channel_id=1, replica_groups=mesh['chan'=32,'day'=8] {'chan'}, use_global_device_ids=true, to_apply=%region_1.1 | all-reduce | flops 8192 | bytes 32768 | tf_op jit(solution)/shard_map/while/body/eval_jaxpr/psum | solution.py:14
  1114.8 104.5 %psum.39 = bf16[1,1,2,4096]{3,2,1,0:T(2,128)(2,1)S(1)} all-reduce(bf16[1,1,2,4096]{3,2,1,0:T(2,128)(2,1)S(1)} %broadcast_select_fusion.2), channel_id=1, replica_groups=mesh['chan'=32,'day'=8] {'chan'}, use_global_device_ids=true, to_apply=%region_1.1 | all-reduce | flops 8192 | bytes 32768 | tf_op jit(solution)/shard_map/while/body/eval_jaxpr/psum | solution.py:14
  1224.5 104.5 %psum.39 = bf16[1,1,2,4096]{3,2,1,0:T(2,128)(2,1)S(1)} all-reduce(bf16[1,1,2,4096]{3,2,1,0:T(2,128)(2,1)S(1)} %broadcast_select_fusion.2), channel_id=1, replica_groups=mesh['chan'=32,'day'=8] {'chan'}, use_global_device_ids=true, to_apply=%region_1.1 | all-reduce | flops 8192 | bytes 32768 | tf_op jit(solution)/shard_map/while/body/eval_jaxpr/psum | solution.py:14
  1334.3 104.5 %psum.39 = bf16[1,1,2,4096]{3,2,1,0:T(2,128)(2,1)S(1)} all-reduce(bf16[1,1,2,4096]{3,2,1,0:T(2,128)(2,1)S(1)} %broadcast_select_fusion.2), channel_id=1, replica_groups=mesh['chan'=32,'day'=8] {'chan'}, use_global_device_ids=true, to_apply=%region_1.1 | all-reduce | flops 8192 | bytes 32768 | tf_op jit(solution)/shard_map/while/body/eval_jaxpr/psum | solution.py:14
  1444.0 104.5 %psum.39 = bf16[1,1,2,4096]{3,2,1,0:T(2,128)(2,1)S(1)} all-reduce(bf16[1,1,2,4096]{3,2,1,0:T(2,128)(2,1)S(1)} %broadcast_select_fusion.2), channel_id=1, replica_groups=mesh['chan'=32,'day'=8] {'chan'}, use_global_device_ids=true, to_apply=%region_1.1 | all-reduce | flops 8192 | bytes 32768 | tf_op jit(solution)/shard_map/while/body/eval_jaxpr/psum | solution.py:14
  1553.7 104.5 %psum.39 = bf16[1,1,2,4096]{3,2,1,0:T(2,128)(2,1)S(1)} all-reduce(bf16[1,1,2,4096]{3,2,1,0:T(2,128)(2,1)S(1)} %broadcast_select_fusion.2), channel_id=1, replica_groups=mesh['chan'=32,'day'=8] {'chan'}, use_global_device_ids=true, to_apply=%region_1.1 | all-reduce | flops 8192 | bytes 32768 | tf_op jit(solution)/shard_map/while/body/eval_jaxpr/psum | solution.py:14
  1663.5 104.5 %psum.39 = bf16[1,1,2,4096]{3,2,1,0:T(2,128)(2,1)S(1)} all-reduce(bf16[1,1,2,4096]{3,2,1,0:T(2,128)(2,1)S(1)} %broadcast_select_fusion.2), channel_id=1, replica_groups=mesh['chan'=32,'day'=8] {'chan'}, use_global_device_ids=true, to_apply=%region_1.1 | all-reduce | flops 8192 | bytes 32768 | tf_op jit(solution)/shard_map/while/body/eval_jaxpr/psum | solution.py:14
  1768.7 17.1 multiply_convert_fusion.1
  1787.6 1.9 fusion.3
  1789.7 85.9 %all-reduce.4.cloned.1.call-done = f32[16,16,256]{2,1,0:T(8,128)} async-done(((f32[16,16,256]{2,1,0:T(8,128)}), f32[16,16,256]{2,1,0:T(8,128)}) %all-reduce.4.cloned.1.call-update) | async-done | bytes 262160 | tf_op jit(solution)/shard_map/psum | solution.py:66
  1875.5 2.1 multiply_reduce_fusion
  1877.8 58.7 %all-reduce.1 = (f32[1,8]{1,0:T(1,128)S(1)}, f32[1,8]{1,0:T(1,128)S(1)}) all-reduce(f32[1,8]{1,0:T(1,128)S(1)} %bitcast.31, f32[1,8]{1,0:T(1,128)S(1)} %bitcast.30), channel_id=1, replica_groups=mesh['chan'=32,'day'=8] {'chan'}, use_global_device_ids=true, to_apply=%region_6.7 | all-reduce | flops 16 | bytes 128 | tf_op jit(solution)/shard_map/psum | solution.py:86
  (66 shorter events, 35.2 us)
Async XLA Ops:
  7.2 1868.4 %all-reduce.4.cloned.1.call-start = ((), (), s32[]{:S(2)}) async-start(), calls=%async_computation | async-start | bytes 524288 | tf_op jit(solution)/shard_map/psum | solution.py:66
  1787.6 2.0 copy-start
  1787.6 90.0 %copy-start.1 = (s32[16]{0:T(128)S(1)}, s32[16]{0:T(128)}, u32[]{:S(2)}) copy-start(s32[16]{0:T(128)} %param.8) | copy-start | bytes 196
Sparse Core Ops, SparseCore 0:
  1789.7 85.8 all-reduce.3
where the time goes:
time: 1950 us; the launch traced here: 1940 us
  blocking collectives  1730 us (89%)
  waiting for transfers between devices  85.9 us (4%)
  loops' own time  52.4 us (3%)
  other arithmetic  34.2 us (2%)
  local copies, waits for them, and re-layouts  22.6 us (1%)
    psum x16, blocking collectives, from_root(): return lax.psum(kept, axis)  1670 us
    psum x1, waiting for transfers between devices, per_device(): total = lax.psum(local_sum, 'day')  85.9 us
    psum x1, blocking collectives, per_device(): lax.psum((jnp.stack(numers, 0), jnp.stack(denoms, 0)), 'chan')  58.7 us
    another operation x1, loops' own time, per_device(): lax.fori_loop(0, nsrc, fetch, jnp.zeros((day_dev, nsrc, 2, bins), jnp.bfl...  52.4 us
  transfers between devices with their start and end apart: 1, of which 1 were waited for; matrix products, arithmetic and copies ran while one was open for 0% of the time, Pallas kernels for 0%

commit v1 on v0

v1 whole, which is shorter than its diff:
```python
import math

import jax
import jax.numpy as jnp
import numpy as np
from jax import lax
from jax.experimental import pallas as pl
from jax.experimental.pallas import tpu as pltpu
from jax.sharding import Mesh, PartitionSpec as P

LAGS = 256
NINT = 8
BINS = 4096
NSRC = 16
CH = 16
LANE = 128
BF = jnp.bfloat16
F32 = jnp.float32
CHUNKS = 8
CB = BINS // CHUNKS
VMEM = pl.BlockSpec(memory_space=pltpu.VMEM)
SMEM = pl.BlockSpec(memory_space=pltpu.SMEM)


def chan_index():
    return (lax.axis_index("z") * 2 + lax.axis_index("xlo")) * 2 + lax.axis_index("core")


def day_index():
    return lax.axis_index("xhi") * 4 + lax.axis_index("y")


def factor_tables():
    tau = np.arange(LAGS, dtype=np.int64)[None, :] - LAGS // 2
    step = np.arange(64, dtype=np.int64)[:, None]
    coarse = math.pi * ((64 * step * tau) % (2 * BINS)) / BINS
    fine = math.pi * ((step * tau) % (2 * BINS)) / BINS
    scale = 1.0 / math.sqrt(BINS)
    parts = [np.cos(coarse) * scale, np.sin(coarse) * scale, np.cos(fine), np.sin(fine)]
    return np.stack(parts).astype(np.float32)


def table_kernel(f_ref, t_ref):
    cb = f_ref[2]
    sb = f_ref[3]
    per = CB // 64

    def body(a, c):
        ca = f_ref[0, pl.ds(a, 1), :]
        sa = f_ref[1, pl.ds(a, 1), :]
        q = a // per
        r = pl.multiple_of((a % per) * 64, 64)
        t_ref[q, pl.ds(r, 64), :] = (ca * cb - sa * sb).astype(BF)
        t_ref[q, pl.ds(CB + r, 64), :] = (-(sa * cb + ca * sb)).astype(BF)
        return c

    lax.fori_loop(0, BINS // 64, body, 0)


def prepare_kernel(src_ref, x_ref, planes_ref, mine_ref, other_ref):
    base = chan_index() * CH
    core = lax.axis_index("core")
    rows = lax.broadcasted_iota(jnp.int32, (64, 32), 0)
    cols = lax.broadcasted_iota(jnp.int32, (64, 32), 1)
    want = jnp.where(rows < 32, 2 * (rows % 16) + (rows // 16) % 2, -1)
    for s in range(NSRC):
        local = src_ref[s] - base
        ok = jnp.logical_and(local >= 0, local < CH)
        first = jnp.where(ok, 2 * local, -1)
        second = jnp.where(ok, 2 * local + 1, -1)
        want = jnp.where(rows == 32 + s, first, want)
        want = jnp.where(rows == 48 + s, second, want)
    pick = (cols == want).astype(F32).astype(BF)
    half = BINS // 2

    def part(h, dst):
        lo = pl.multiple_of(h * half, half)
        for g in range(half // 512):
            off = pl.multiple_of(lo + g * 512, 512)
            got = jnp.dot(pick, x_ref[:, pl.ds(off, 512)], preferred_element_type=F32)
            planes_ref[:, pl.ds(off, 512)] = got[:32]
            srcs = got[32:].astype(BF)
            for j in range(4):
                dst[g * 4 + j] = srcs[:, j * LANE : (j + 1) * LANE]

    part(1 - core, other_ref)
    part(core, mine_ref)


def spread_kernel(p_ref, o_ref):
    n = p_ref.shape[0]
    total = p_ref[0]
    for i in range(1, n):
        total = total + p_ref[i]
    for i in range(n):
        o_ref[i] = total


def correlate_kernel(planes_ref, mine_ref, other_ref, t_ref, o_ref, cross_ref):
    core = lax.axis_index("core")

    def build(v_ref, slot, g, off):
        for j in range(CB // LANE):
            lo = pl.multiple_of(off + j * LANE, LANE)
            sr = planes_ref[0:16, pl.ds(lo, LANE)]
            si = planes_ref[16:32, pl.ds(lo, LANE)]
            v = v_ref[g * (CB // LANE) + j].astype(F32)
            for s in range(NSRC):
                vr = v[s : s + 1]
                vi = v[16 + s : 17 + s]
                cross_ref[slot, s * CH : (s + 1) * CH, j * LANE : (j + 1) * LANE] = (
                    sr * vr + si * vi
                ).astype(BF)
                cross_ref[slot, s * CH : (s + 1) * CH, CB + j * LANE : CB + (j + 1) * LANE] = (
                    si * vr - sr * vi
                ).astype(BF)

    per_half = CHUNKS // 2
    o_ref[...] = jnp.zeros_like(o_ref)
    for v_ref, h in ((mine_ref, core), (other_ref, 1 - core)):

        def body(g, c, v_ref=v_ref, h=h):
            q = h * per_half + g
            build(v_ref, 0, g, q * CB)
            o_ref[...] += jnp.dot(cross_ref[0], t_ref[q], preferred_element_type=F32)
            return c

        lax.fori_loop(0, per_half, body, 0)


def drift_kernel(bounds_ref, intr_ref, c_ref, ref_ref, o_ref):
    day = day_index()
    lane = lax.broadcasted_iota(jnp.int32, (32, LAGS), 1)
    rowi = lax.broadcasted_iota(jnp.int32, (32, LAGS), 0)
    first = jnp.where(rowi < 16, bounds_ref[2 * day, 0], bounds_ref[2 * day + 1, 0])
    last = jnp.where(rowi < 16, bounds_ref[2 * day, 1], bounds_ref[2 * day + 1, 1])
    window = jnp.logical_and(lane >= first, lane < last)
    not_last = lane < LAGS - 1
    not_first = lane > 0
    rows = lax.broadcasted_iota(jnp.int32, (32, LANE), 0) % 16
    cols = lax.broadcasted_iota(jnp.int32, (32, LANE), 1)
    kind = jnp.zeros((32, LANE), jnp.int32)
    for c in range(CH):
        kind = jnp.where(rows == c, intr_ref[c], kind)
    in_num = (cols == kind).astype(F32)
    in_den = (cols == kind + NINT).astype(F32)
    total = c_ref[0]
    for d in range(1, 8):
        total = total + c_ref[d]
    ref = (total * 0.125).astype(BF)
    ref_ref[...] = ref
    ref = ref.astype(F32)
    for d in range(8):
        corr = c_ref[d]
        ahead = jnp.where(not_last, pltpu.roll(corr, LAGS - 1, 1), 0.0)
        behind = jnp.where(not_first, pltpu.roll(corr, 1, 1), 0.0)
        slope = jnp.where(window, 0.5 * (ahead - behind), 0.0)
        num = jnp.sum(slope * (corr - ref), axis=1, keepdims=True)
        den = jnp.sum(slope * slope, axis=1, keepdims=True)
        o_ref[d] = jnp.sum(num * in_num + den * in_den, axis=0, keepdims=True)


def repeat_sum_kernel(p_ref, o_ref):
    total = jnp.sum(p_ref[...], axis=0)
    for i in range(o_ref.shape[0]):
        o_ref[i] = total


def finish_kernel(p_ref, o_ref):
    total = jnp.sum(p_ref[...], axis=0)
    o_ref[...] = total[:, :NINT] / (total[:, NINT : 2 * NINT] + 1e-06)


def call(kernel, out_shape, in_specs, name, scratch=()):
    multi = isinstance(out_shape, (list, tuple))
    return pl.pallas_call(
        kernel,
        out_shape=out_shape,
        in_specs=in_specs,
        out_specs=[VMEM] * len(out_shape) if multi else VMEM,
        scratch_shapes=list(scratch),
        compiler_params=pltpu.CompilerParams(vmem_limit_bytes=40 << 20),
        name=name,
    )


def shaped(shape, dtype):
    return jax.ShapeDtypeStruct(shape, dtype)


PAIR = [(0, 1), (1, 0)]


def per_device(spectra, source_index, interrogator, lag_bounds):
    x = spectra.reshape(2 * CH, BINS)
    piece = (16, 32, LANE)
    table = call(table_kernel, shaped((CHUNKS, 2 * CB, LAGS), BF), [VMEM], "lag_table")(
        jnp.asarray(factor_tables())
    )
    planes, mine, other = call(
        prepare_kernel,
        [shaped((32, BINS), F32), shaped(piece, BF), shaped(piece, BF)],
        [SMEM, VMEM],
        "prepare",
    )(source_index, x)
    got = lax.ppermute(other, "core", PAIR)
    parts = lax.all_to_all(mine + got, ("z", "xlo"), 0, 0)
    parts = call(spread_kernel, shaped(piece, BF), [VMEM], "spread")(parts)
    mine_half = lax.all_to_all(parts, ("z", "xlo"), 0, 0)
    other_half = lax.ppermute(mine_half, "core", PAIR)
    corr = call(
        correlate_kernel,
        shaped((NSRC * CH, LAGS), F32),
        [VMEM] * 4,
        "correlate",
        [pltpu.VMEM((1, NSRC * CH, 2 * CB), BF)],
    )(planes, mine_half, other_half, table)
    days = lax.all_to_all(corr.reshape(8, 32, LAGS), ("xhi", "y"), 0, 0)
    ref, fits = call(
        drift_kernel,
        [shaped((32, LAGS), BF), shaped((8, 1, LANE), F32)],
        [SMEM, SMEM, VMEM],
        "drift",
    )(lag_bounds, interrogator, days)
    fits = lax.all_to_all(fits, ("xhi", "y"), 0, 0)
    fits = call(repeat_sum_kernel, shaped((32, 1, LANE), F32), [VMEM], "day_fits")(fits)
    fits = lax.all_to_all(fits, ("z", "xlo", "core"), 0, 0)
    drift = call(finish_kernel, shaped((1, NINT), F32), [VMEM], "finish")(fits)
    return ref.reshape(2, CH, LAGS), drift


def solution(mesh):
    fine = Mesh(mesh.devices.reshape(8, 2, 2, 2, 4), ("z", "xlo", "core", "xhi", "y"))
    chan = ("z", "xlo", "core")
    day = ("xhi", "y")
    return jax.shard_map(
        per_device,
        mesh=fine,
        in_specs=(P(day, chan, None, None), P(), P(chan), P()),
        out_specs=(P(day, chan, None), P(day, None)),
        check_vma=False,
    )
```

time: 1950 us -> 83.7 us (0.04)
  blocking collectives: 1730 us -> 50 us
  waiting for transfers between devices: 85.9 us -> 8.49 us
  loops' own time: 52.4 us -> 0 us
  other arithmetic: 34.2 us -> 0.04 us
  local copies, waits for them, and re-layouts: 22.6 us -> 2.74 us
    psum x17 -> x0, blocking collectives: 1730 us -> none  [the longest x16 1670 us: from_root(): return lax.psum(kept, axis)]
    psum x1 -> x0, waiting for transfers between devices: 85.9 us -> none  [per_device(): total = lax.psum(local_sum, 'day')]
    another operation x1 -> x0, loops' own time: 52.4 us -> none  [per_device(): lax.fori_loop(0, nsrc, fetch, jnp.zeros((day_dev, nsrc, 2, bins), jnp.bfl...]
    all_to_all x0 -> x4, blocking collectives: none -> 50 us  [the longest x1 15.8 us: per_device(): parts = lax.all_to_all(mine + got, ('z', 'xlo'), 0, 0)]
    dynamic_slice x17 -> x0, local copies, waits for them, and re-layouts: 20.5 us -> none  [the longest x16 19.9 us: fetch(): chosen_chan = source_index[source]]
  transfers between devices with their start and end apart: 1 -> 3, of which waited for: 1 -> 2; matrix products, arithmetic and copies ran while one was open for 0% -> 0% of each run, Pallas kernels for 0% -> 2%
where the time goes in v1:
time: 83.7 us; the launch traced here: 83.3 us
  blocking collectives  50 us (60%)
  starting transfers between devices  12.7 us (15%)
  Pallas kernels  8.71 us (10%)
  waiting for transfers between devices  8.49 us (10%)
  local copies, waits for them, and re-layouts  2.74 us (3%)
    all_to_all x1, blocking collectives, per_device(): parts = lax.all_to_all(mine + got, ('z', 'xlo'), 0, 0)  15.8 us
    all_to_all x1, blocking collectives, per_device(): fits = lax.all_to_all(fits, ('z', 'xlo', 'core'), 0, 0)  12.5 us
    all_to_all x1, blocking collectives, per_device(): mine_half = lax.all_to_all(parts, ('z', 'xlo'), 0, 0)  11.2 us
    all_to_all x1, blocking collectives, per_device(): fits = lax.all_to_all(fits, ('xhi', 'y'), 0, 0)  10.4 us
    all_to_all x1, waiting for transfers between devices, per_device(): days = lax.all_to_all(corr.reshape(8, 32, LAGS), ('xhi', 'y'), 0, 0)  7.5 us
    all_to_all x1, starting transfers between devices, per_device(): days = lax.all_to_all(corr.reshape(8, 32, LAGS), ('xhi', 'y'), 0, 0)  6.35 us
    pallas_call x1, Pallas kernels, per_device(): call(correlate_kernel, shaped((NSRC * CH, LAGS), F32), [VMEM] * 4, 'corre...  3.84 us
    ppermute x1, starting transfers between devices, per_device(): got = lax.ppermute(other, 'core', PAIR)  3.29 us
  transfers between devices with their start and end apart: 3, of which 2 were waited for; matrix products, arithmetic and copies ran while one was open for 0% of the time, Pallas kernels for 2%

profile of v1, /device:TPU:1, one launch (start us, length us, event | category | flops | bytes accessed | tf_op | source)
XLA Modules:
  0.0 83.3 jit_solution(14001317725968129073)
XLA Ops:
  0.6 1.0 %reshape.13.x_ref = bf16[32,4096]{1,0:T(8,128)(2,1)S(1)} reshape(bf16[1,16,2,4096]{3,2,1,0:T(2,128)(2,1)} %param.5) | data formatting | bytes 524288 | tf_op jit(solution)/shard_map/reshape | solution.py:195
  1.7 0.0 copy-start.1
  1.7 0.6 copy-done.1
  2.3 0.9 %prepare.1 = (f32[32,4096]{1,0:T(8,128)S(1)}, bf16[16,32,128]{2,1,0:T(8,128)(2,1)S(1)}, bf16[16,32,128]{2,1,0:T(8,128)(2,1)S(1)}) custom-call(s32[16]{0:T(128)S(1)} %copy-done.1, bf16[32,4096]{1,0:T(8,128)(2,1)S(1)} %reshape.13.x_ref), custom_call_target="tpu_custom_call" | custom-call | tf_op jit(solution)/shard_map/prepare/pallas_call | solution.py:200
  3.2 3.3 %collective-permute-start = (bf16[16,32,128]{2,1,0:T(8,128)(2,1)S(1)}, bf16[16,32,128]{2,1,0:T(8,128)(2,1)S(1)}, u32[]{:S(2)}, u32[]{:S(2)}) collective-permute-start(bf16[16,32,128]{2,1,0:T(8,128)(2,1)S(1)} %get-tuple-element.9), channel_id=1, source_target_pairs={{0,8},{8,0},{1,9},{9,1},{2,10},{10,2},{3,11},{11,3},{4,12},{12,4},... | collective-permute-start | bytes 393224 | tf_op jit(solution)/shard_map/ppermute | solution.py:206
  6.5 1.0 %collective-permute-done = bf16[16,32,128]{2,1,0:T(8,128)(2,1)S(1)} collective-permute-done((bf16[16,32,128]{2,1,0:T(8,128)(2,1)S(1)}, bf16[16,32,128]{2,1,0:T(8,128)(2,1)S(1)}, u32[]{:S(2)}, u32[]{:S(2)}) %collective-permute-start) | collective-permute-done | bytes 131104 | tf_op jit(solution)/shard_map/ppermute | solution.py:206
  7.5 15.8 %all_to_all.25.p_ref = bf16[16,32,128]{2,1,0:T(8,128)(2,1)S(1)} all-to-all(bf16[16,32,128]{2,1,0:T(8,128)(2,1)S(1)} %add.3), channel_id=1, replica_groups=mesh['z'=8,'xlo'=2,'core'=2,'xhi'=2,'y'=4] {'z','xlo'}, dimensions={0} | all-to-all | bytes 262144 | tf_op jit(solution)/shard_map/all_to_all | solution.py:207
  23.4 11.2 %all_to_all.26.mine_ref = bf16[16,32,128]{2,1,0:T(8,128)(2,1)S(1)} all-to-all(bf16[16,32,128]{2,1,0:T(8,128)(2,1)S(1)} %spread.1), channel_id=1, replica_groups=mesh['z'=8,'xlo'=2,'core'=2,'xhi'=2,'y'=4] {'z','xlo'}, dimensions={0} | all-to-all | bytes 262144 | tf_op jit(solution)/shard_map/all_to_all | solution.py:209
  34.5 3.0 %collective-permute-start.1 = (bf16[16,32,128]{2,1,0:T(8,128)(2,1)S(1)}, bf16[16,32,128]{2,1,0:T(8,128)(2,1)S(1)}, u32[]{:S(2)}, u32[]{:S(2)}) collective-permute-start(bf16[16,32,128]{2,1,0:T(8,128)(2,1)S(1)} %all_to_all.26.mine_ref), channel_id=1, source_target_pairs={{0,8},{8,0},{1,9},{9,1},{2,10},{10,2},{3,11},{11,3},{4,12},{12,4},... | collective-permute-start | bytes 393224 | tf_op jit(solution)/shard_map/ppermute | solution.py:210
  37.6 0.0 copy-start
  37.6 0.9 %copy-done = f32[4,64,256]{2,1,0:T(8,128)S(1)} copy-done((f32[4,64,256]{2,1,0:T(8,128)S(1)}, f32[4,64,256]{2,1,0:T(8,128)}, u32[]{:S(2)}) %copy-start) | copy-done | bytes 262168
  38.5 0.0 copy-start.3
  38.5 1.5 %lag_table.1.t_ref = bf16[8,1024,256]{2,1,0:T(8,128)(2,1)S(1)} custom-call(f32[4,64,256]{2,1,0:T(8,128)S(1)} %copy-done), custom_call_target="tpu_custom_call" | custom-call | tf_op jit(solution)/shard_map/lag_table/pallas_call | solution.py:197
  40.0 0.0 collective-permute-done.1.other_ref
  40.0 3.8 %correlate.1 = f32[256,256]{1,0:T(8,128)} custom-call(f32[32,4096]{1,0:T(8,128)S(1)} %get-tuple-element.7.planes_ref, bf16[16,32,128]{2,1,0:T(8,128)(2,1)S(1)} %all_to_all.26.mine_ref, bf16[16,32,128]{2,1,0:T(8,128)(2,1)S(1)} %collective-permute-done.1.other_ref, bf16[8,1024,256]{2,1,0:T(8,128)(2,1)S(1)} %lag_table.1.t_ref), custom_call_target="tpu_custom_call" | custom-call | tf_op jit(solution)/shard_map/correlate/pallas_call | solution.py:211
  43.8 6.4 %all-to-all-start.2 = ((f32[8,32,256]{2,1,0:T(8,128)}), f32[8,32,256]{2,1,0:T(8,128)S(1)}, u32[]{:S(2)}, u32[]{:S(2)}) async-start(f32[8,32,256]{2,1,0:T(8,128)} %bitcast), calls=%async_computation.2 | async-start | bytes 524288 | tf_op jit(solution)/shard_map/all_to_all | solution.py:218
  50.2 0.0 copy-done.3
  50.2 0.1 copy.7.bounds_ref
  50.3 7.5 %all-to-all-done.2.c_ref = f32[8,32,256]{2,1,0:T(8,128)S(1)} async-done(((f32[8,32,256]{2,1,0:T(8,128)}), f32[8,32,256]{2,1,0:T(8,128)S(1)}, u32[]{:S(2)}, u32[]{:S(2)}) %all-to-all-start.2) | async-done | bytes 262176 | tf_op jit(solution)/shard_map/all_to_all | solution.py:218
  57.8 0.0 copy-done.2
  57.8 1.9 %drift.1 = (bf16[32,256]{1,0:T(8,128)(2,1)}, f32[8,1,128]{2,1,0:T(1,128)S(1)}) custom-call(s32[16,2]{1,0:T(8,128)S(1)} %copy.7.bounds_ref, s32[16]{0:T(128)S(1)} %copy-done.2, f32[8,32,256]{2,1,0:T(8,128)S(1)} %all-to-all-done.2.c_ref), custom_call_target="tpu_custom_call" | custom-call | tf_op jit(solution)/shard_map/drift/pallas_call | solution.py:219
  59.7 10.4 %all_to_all.27.p_ref = f32[8,1,128]{2,1,0:T(1,128)S(1)} all-to-all(f32[8,1,128]{2,1,0:T(1,128)S(1)} %get-tuple-element.11), channel_id=1, replica_groups=mesh['z'=8,'xlo'=2,'core'=2,'xhi'=2,'y'=4] {'xhi','y'}, dimensions={0} | all-to-all | bytes 8192 | tf_op jit(solution)/shard_map/all_to_all | solution.py:225
  70.2 12.5 %all_to_all.28.p_ref = f32[32,1,128]{2,1,0:T(1,128)S(1)} all-to-all(f32[32,1,128]{2,1,0:T(1,128)S(1)} %day_fits.1), channel_id=1, replica_groups=mesh['z'=8,'xlo'=2,'core'=2,'xhi'=2,'y'=4] {'z','xlo','core'}, dimensions={0} | all-to-all | bytes 32768 | tf_op jit(solution)/shard_map/all_to_all | solution.py:227
  82.7 0.6 finish.1
  (4 shorter events, 0.1 us)
Async XLA Ops:
  1.7 0.7 copy-start.1
  3.2 4.3 %collective-permute-start = (bf16[16,32,128]{2,1,0:T(8,128)(2,1)S(1)}, bf16[16,32,128]{2,1,0:T(8,128)(2,1)S(1)}, u32[]{:S(2)}, u32[]{:S(2)}) collective-permute-start(bf16[16,32,128]{2,1,0:T(8,128)(2,1)S(1)} %get-tuple-element.9), channel_id=1, source_target_pairs={{0,8},{8,0},{1,9},{9,1},{2,10},{10,2},{3,11},{11,3},{4,12},{12,4},... | collective-permute-start | bytes 393224 | tf_op jit(solution)/shard_map/ppermute | solution.py:206
  34.5 5.4 %collective-permute-start.1 = (bf16[16,32,128]{2,1,0:T(8,128)(2,1)S(1)}, bf16[16,32,128]{2,1,0:T(8,128)(2,1)S(1)}, u32[]{:S(2)}, u32[]{:S(2)}) collective-permute-start(bf16[16,32,128]{2,1,0:T(8,128)(2,1)S(1)} %all_to_all.26.mine_ref), channel_id=1, source_target_pairs={{0,8},{8,0},{1,9},{9,1},{2,10},{10,2},{3,11},{11,3},{4,12},{12,4},... | collective-permute-start | bytes 393224 | tf_op jit(solution)/shard_map/ppermute | solution.py:210
  37.6 0.9 %copy-start = (f32[4,64,256]{2,1,0:T(8,128)S(1)}, f32[4,64,256]{2,1,0:T(8,128)}, u32[]{:S(2)}) copy-start(f32[4,64,256]{2,1,0:T(8,128)} %constant.2.clone.f_ref) | copy-start | bytes 786436
  38.5 11.7 %copy-start.3 = (s32[16,2]{0,1:T(2,128)S(1)}, s32[16,2]{0,1:T(2,128)}, u32[]{:S(2)}) copy-start(s32[16,2]{0,1:T(2,128)} %param.8) | copy-start | bytes 388
  38.5 19.3 %copy-start.2 = (s32[16]{0:T(128)S(1)}, s32[16]{0:T(128)}, u32[]{:S(2)}) copy-start(s32[16]{0:T(128)} %intr_ref.1) | copy-start | bytes 196
  43.8 13.9 %all-to-all-start.2 = ((f32[8,32,256]{2,1,0:T(8,128)}), f32[8,32,256]{2,1,0:T(8,128)S(1)}, u32[]{:S(2)}, u32[]{:S(2)}) async-start(f32[8,32,256]{2,1,0:T(8,128)} %bitcast), calls=%async_computation.2 | async-start | bytes 524288 | tf_op jit(solution)/shard_map/all_to_all | solution.py:218

commit v2 on v1

v2 whole, which is shorter than its diff:
```python
import math

import jax
import jax.numpy as jnp
import numpy as np
from jax import lax
from jax.experimental import pallas as pl
from jax.experimental.pallas import tpu as pltpu
from jax.sharding import Mesh, PartitionSpec as P

LAGS = 256
NINT = 8
BINS = 4096
NSRC = 16
CH = 16
LANE = 128
BF = jnp.bfloat16
F32 = jnp.float32
CHUNKS = 8
CB = BINS // CHUNKS
VMEM = pl.BlockSpec(memory_space=pltpu.VMEM)
SMEM = pl.BlockSpec(memory_space=pltpu.SMEM)


def chan_index():
    return (lax.axis_index("z") * 2 + lax.axis_index("xlo")) * 2 + lax.axis_index("core")


def day_index():
    return lax.axis_index("xhi") * 4 + lax.axis_index("y")


def factor_tables():
    tau = np.arange(LAGS, dtype=np.int64)[None, :] - LAGS // 2
    step = np.arange(64, dtype=np.int64)[:, None]
    coarse = math.pi * ((64 * step * tau) % (2 * BINS)) / BINS
    fine = math.pi * ((step * tau) % (2 * BINS)) / BINS
    scale = 1.0 / math.sqrt(BINS)
    parts = [np.cos(coarse) * scale, np.sin(coarse) * scale, np.cos(fine), np.sin(fine)]
    return np.stack(parts).astype(np.float32)


def table_kernel(f_ref, _, t_ref):
    cb = f_ref[2]
    sb = f_ref[3]
    per = CB // 64

    def body(a, c):
        ca = f_ref[0, pl.ds(a, 1), :]
        sa = f_ref[1, pl.ds(a, 1), :]
        q = a // per
        r = pl.multiple_of((a % per) * 64, 64)
        t_ref[q, pl.ds(r, 64), :] = (ca * cb - sa * sb).astype(BF)
        t_ref[q, pl.ds(CB + r, 64), :] = (-(sa * cb + ca * sb)).astype(BF)
        return c

    lax.fori_loop(0, BINS // 64, body, 0)


def prepare_kernel(
    spec_hbm,
    src_hbm,
    intr_hbm,
    bounds_hbm,
    f_hbm,
    planes_ref,
    mine_ref,
    other_ref,
    window_ref,
    member_ref,
    f_ref,
    x_ref,
    src_ref,
    intr_ref,
    bounds_ref,
    sems,
):
    copies = [
        pltpu.make_async_copy(a, b, sems.at[i])
        for i, (a, b) in enumerate(
            (
                (src_hbm, src_ref),
                (spec_hbm, x_ref),
                (intr_hbm, intr_ref),
                (bounds_hbm, bounds_ref),
                (f_hbm, f_ref),
            )
        )
    ]
    for copy in copies:
        copy.start()
    base = chan_index() * CH
    core = lax.axis_index("core")
    rows = lax.broadcasted_iota(jnp.int32, (64, 32), 0)
    cols = lax.broadcasted_iota(jnp.int32, (64, 32), 1)
    want = jnp.where(rows < 32, 2 * (rows % 16) + (rows // 16) % 2, -1)
    copies[0].wait()
    for s in range(NSRC):
        local = src_ref[s] - base
        ok = jnp.logical_and(local >= 0, local < CH)
        first = jnp.where(ok, 2 * local, -1)
        second = jnp.where(ok, 2 * local + 1, -1)
        want = jnp.where(rows == 32 + s, first, want)
        want = jnp.where(rows == 48 + s, second, want)
    pick = (cols == want).astype(F32).astype(BF)
    half = BINS // 2
    copies[1].wait()

    def part(h, dst):
        lo = pl.multiple_of(h * half, half)
        for g in range(half // 512):
            off = pl.multiple_of(lo + g * 512, 512)
            x = x_ref[:, :, pl.ds(off, 512)].reshape(2 * CH, 512)
            got = jnp.dot(pick, x, preferred_element_type=F32)
            planes_ref[:, pl.ds(off, 512)] = got[:32]
            srcs = got[32:].astype(BF)
            for j in range(4):
                dst[g * 4 + j] = srcs[:, j * LANE : (j + 1) * LANE]

    part(1 - core, other_ref)
    part(core, mine_ref)

    copies[2].wait()
    copies[3].wait()
    day = day_index()
    lane = lax.broadcasted_iota(jnp.int32, (32, LAGS), 1)
    rowi = lax.broadcasted_iota(jnp.int32, (32, LAGS), 0)
    first = jnp.where(rowi < CH, bounds_ref[0, 2 * day], bounds_ref[0, 2 * day + 1])
    last = jnp.where(rowi < CH, bounds_ref[1, 2 * day], bounds_ref[1, 2 * day + 1])
    window_ref[...] = jnp.logical_and(lane >= first, lane < last).astype(F32)
    rows = lax.broadcasted_iota(jnp.int32, (32, LANE), 0) % CH
    cols = lax.broadcasted_iota(jnp.int32, (32, LANE), 1)
    kind = jnp.zeros((32, LANE), jnp.int32)
    for c in range(CH):
        kind = jnp.where(rows == c, intr_ref[c], kind)
    member_ref[0] = (cols == kind).astype(F32)
    member_ref[1] = (cols == kind + NINT).astype(F32)
    copies[4].wait()


def spread_kernel(p_ref, o_ref):
    n = p_ref.shape[0]
    total = p_ref[0]
    for i in range(1, n):
        total = total + p_ref[i]
    for i in range(n):
        o_ref[i] = total


def build_cross(planes_ref, v_ref, cross_ref, g, off):
    for j in range(CB // LANE):
        lo = pl.multiple_of(off + j * LANE, LANE)
        sr = planes_ref[0:16, pl.ds(lo, LANE)]
        si = planes_ref[16:32, pl.ds(lo, LANE)]
        v = v_ref[g * (CB // LANE) + j].astype(F32)
        for s in range(NSRC):
            vr = v[s : s + 1]
            vi = v[16 + s : 17 + s]
            cross_ref[s * CH : (s + 1) * CH, j * LANE : (j + 1) * LANE] = (
                sr * vr + si * vi
            ).astype(BF)
            cross_ref[s * CH : (s + 1) * CH, CB + j * LANE : CB + (j + 1) * LANE] = (
                si * vr - sr * vi
            ).astype(BF)


def half_correlation(planes_ref, v_ref, t_ref, crosses, half):
    per_half = CHUNKS // 2
    total = None
    build_cross(planes_ref, v_ref, crosses[0], 0, half * per_half * CB)
    for g in range(per_half):
        q = half * per_half + g
        if g + 1 < per_half:
            build_cross(planes_ref, v_ref, crosses[(g + 1) % 2], g + 1, (q + 1) * CB)
        got = jnp.dot(crosses[g % 2][...], t_ref[q], preferred_element_type=F32)
        total = got if total is None else total + got
    return total


def first_half_kernel(planes_ref, v_ref, t_ref, o_ref, cross_a, cross_b):
    core = lax.axis_index("core")
    o_ref[...] = half_correlation(planes_ref, v_ref, t_ref, (cross_a, cross_b), core)


def second_half_kernel(planes_ref, v_ref, t_ref, first_ref, o_ref, cross_a, cross_b):
    core = lax.axis_index("core")
    total = half_correlation(planes_ref, v_ref, t_ref, (cross_a, cross_b), 1 - core)
    o_ref[...] = (first_ref[...] + total).reshape(o_ref.shape)


def drift_kernel(window_ref, member_ref, c_ref, ref_ref, o_ref):
    lane = lax.broadcasted_iota(jnp.int32, (32, LAGS), 1)
    window = window_ref[...] * 0.5
    ahead_w = jnp.where(lane < LAGS - 1, window, 0.0)
    behind_w = jnp.where(lane > 0, window, 0.0)
    in_num = member_ref[0]
    in_den = member_ref[1]
    total = c_ref[0]
    for d in range(1, 8):
        total = total + c_ref[d]
    ref = (total * 0.125).astype(BF)
    ref_ref[...] = ref
    ref = ref.astype(F32)
    for d in range(8):
        corr = c_ref[d]
        slope = pltpu.roll(corr, LAGS - 1, 1) * ahead_w - pltpu.roll(corr, 1, 1) * behind_w
        num = jnp.sum(slope * (corr - ref), axis=1, keepdims=True)
        den = jnp.sum(slope * slope, axis=1, keepdims=True)
        row = jnp.sum(num * in_num + den * in_den, axis=0, keepdims=True)
        for i in range(4):
            o_ref[d // 4, i, d % 4] = jnp.broadcast_to(row, (8, LANE))


def repeat_sum_kernel(p_ref, o_ref):
    total = jnp.sum(p_ref[...], axis=0)[:1]
    for i in range(o_ref.shape[0]):
        o_ref[i] = total


def finish_kernel(p_ref, r_ref, ref_ref, o_ref):
    ref_ref[...] = r_ref[...]
    total = jnp.sum(p_ref[...], axis=0)
    o_ref[...] = total[:, :NINT] / (total[:, NINT : 2 * NINT] + 1e-06)


def call(kernel, out_shape, in_specs, name, scratch=()):
    multi = isinstance(out_shape, (list, tuple))
    return pl.pallas_call(
        kernel,
        out_shape=out_shape,
        in_specs=in_specs,
        out_specs=[VMEM] * len(out_shape) if multi else VMEM,
        scratch_shapes=list(scratch),
        compiler_params=pltpu.CompilerParams(vmem_limit_bytes=40 << 20),
        name=name,
    )


def shaped(shape, dtype):
    return jax.ShapeDtypeStruct(shape, dtype)


PAIR = [(0, 1), (1, 0)]


def per_device(spectra, source_index, interrogator, lag_bounds):
    piece = (16, 32, LANE)
    factors = factor_tables()
    hbm = pl.BlockSpec(memory_space=pltpu.HBM)
    anywhere = pl.BlockSpec(memory_space=pl.ANY)
    planes, mine, other, window, member, factors = call(
        prepare_kernel,
        [
            shaped((32, BINS), F32),
            shaped(piece, BF),
            shaped(piece, BF),
            shaped((32, LAGS), F32),
            shaped((2, 32, LANE), F32),
            shaped(factors.shape, F32),
        ],
        [hbm] * 5,
        "prepare",
        [
            pltpu.VMEM((CH, 2, BINS), BF),
            pltpu.SMEM((NSRC,), jnp.int32),
            pltpu.SMEM((CH,), jnp.int32),
            pltpu.SMEM((2, NSRC), jnp.int32),
            pltpu.SemaphoreType.DMA((5,)),
        ],
    )(
        *(
            pltpu.with_memory_space_constraint(a, pltpu.HBM)
            for a in (
                spectra.reshape(CH, 2, BINS),
                source_index,
                interrogator,
                lag_bounds.T,
                jnp.asarray(factors),
            )
        )
    )
    got = lax.ppermute(other, "core", PAIR)
    table = call(
        table_kernel, shaped((CHUNKS, 2 * CB, LAGS), BF), [VMEM, anywhere], "lag_table"
    )(factors, planes)
    got, table = lax.optimization_barrier((got, table))
    parts = lax.all_to_all(mine + got, ("z", "xlo"), 0, 0)
    parts = call(spread_kernel, shaped(piece, BF), [VMEM], "spread")(parts)
    mine_half = lax.all_to_all(parts, ("z", "xlo"), 0, 0)
    other_half = lax.ppermute(mine_half, "core", PAIR)
    crosses = [pltpu.VMEM((NSRC * CH, 2 * CB), BF)] * 2
    first = call(
        first_half_kernel, shaped((NSRC * CH, LAGS), F32), [VMEM] * 3, "first_half", crosses
    )(planes, mine_half, table)
    corr = call(
        second_half_kernel, shaped((8, 32, LAGS), F32), [VMEM] * 4, "second_half", crosses
    )(planes, other_half, table, first)
    days = lax.all_to_all(corr, ("xhi", "y"), 0, 0)
    ref, fits = call(
        drift_kernel,
        [shaped((32, LAGS), BF), shaped((2, 4, 4, 8, LANE), F32)],
        [VMEM] * 3,
        "drift",
    )(window, member, days)
    fits = lax.all_to_all(fits.reshape(32, 8, LANE), ("xhi", "xlo", "core", "y"), 0, 0)
    fits = call(repeat_sum_kernel, shaped((8, 1, LANE), F32), [VMEM], "near_fits")(fits)
    fits = lax.all_to_all(fits, "z", 0, 0)
    ref, drift = call(
        finish_kernel,
        [shaped((32, LAGS), BF), shaped((1, NINT), F32)],
        [VMEM] * 2,
        "finish",
    )(fits, ref)
    return ref.reshape(2, CH, LAGS), drift


def solution(mesh):
    fine = Mesh(mesh.devices.reshape(8, 2, 2, 2, 4), ("z", "xlo", "core", "xhi", "y"))
    chan = ("z", "xlo", "core")
    day = ("xhi", "y")
    return jax.shard_map(
        per_device,
        mesh=fine,
        in_specs=(P(day, chan, None, None), P(), P(chan), P()),
        out_specs=(P(day, chan, None), P(day, None)),
        check_vma=False,
    )
```

time: 83.7 us -> 76.6 us (0.915)
  blocking collectives: 50 us -> 62.4 us
  waiting for transfers between devices: 8.49 us -> 0.01 us
  starting transfers between devices: 12.7 us -> 6.12 us
  local copies, waits for them, and re-layouts: 2.74 us -> 0 us
  Pallas kernels: 8.71 us -> 7.05 us
    all_to_all x2 -> x3, blocking collectives: 23 us -> 35.1 us  [the longest x1 13.7 us: per_device(): days = lax.all_to_all(corr, ('xhi', 'y'), 0, 0)]
    all_to_all x1 -> x0, waiting for transfers between devices: 7.5 us -> none  [per_device(): days = lax.all_to_all(corr.reshape(8, 32, LAGS), ('xhi', 'y'), 0, 0)]
    all_to_all x1 -> x0, starting transfers between devices: 6.35 us -> none  [per_device(): days = lax.all_to_all(corr.reshape(8, 32, LAGS), ('xhi', 'y'), 0, 0)]
    pallas_call x5 -> x6, Pallas kernels: 7.82 us -> 5.69 us  [the longest x1 1.45 us: per_device(): call(table_kernel, shaped((CHUNKS, 2 * CB, LAGS), BF), [VMEM, anywhere],...]
    unnamed x9 -> x0, local copies, waits for them, and re-layouts: 1.69 us -> none
    reshape x1 -> x0, local copies, waits for them, and re-layouts: 1.05 us -> none  [per_device(): x = spectra.reshape(2 * CH, BINS)]
    ppermute x1, waiting for transfers between devices: 0.99 us -> 0.01 us  [per_device(): got = lax.ppermute(other, 'core', PAIR)]
  transfers between devices with their start and end apart: 3 -> 2, of which waited for: 2 -> 0; matrix products, arithmetic and copies ran while one was open for 0% -> 0% of each run, Pallas kernels for 2% -> 4%
where the time goes in v2:
time: 76.6 us; the launch traced here: 76.3 us
  blocking collectives  62.4 us (81%)
  Pallas kernels  7.05 us (9%)
  starting transfers between devices  6.12 us (8%)
    all_to_all x1, blocking collectives, per_device(): parts = lax.all_to_all(mine + got, ('z', 'xlo'), 0, 0)  16.1 us
    all_to_all x1, blocking collectives, per_device(): days = lax.all_to_all(corr, ('xhi', 'y'), 0, 0)  13.7 us
    all_to_all x1, blocking collectives, per_device(): lax.all_to_all(fits.reshape(32, 8, LANE), ('xhi', 'xlo', 'core', 'y'), 0, 0)  12.4 us
    all_to_all x1, blocking collectives, per_device(): mine_half = lax.all_to_all(parts, ('z', 'xlo'), 0, 0)  11.2 us
    all_to_all x1, blocking collectives, per_device(): fits = lax.all_to_all(fits, 'z', 0, 0)  8.92 us
    ppermute x1, starting transfers between devices, per_device(): got = lax.ppermute(other, 'core', PAIR)  3.29 us
    ppermute x1, starting transfers between devices, per_device(): other_half = lax.ppermute(mine_half, 'core', PAIR)  2.84 us
  transfers between devices with their start and end apart: 2, of which 0 were waited for; matrix products, arithmetic and copies ran while one was open for 0% of the time, Pallas kernels for 4%

profile of v2, /device:TPU:1, one launch (start us, length us, event | category | flops | bytes accessed | tf_op | source)
XLA Modules:
  0.0 76.3 jit_solution(9081769228869983247)
XLA Ops:
  0.6 1.3 %prepare.1 = (f32[32,4096]{1,0:T(8,128)S(1)}, bf16[16,32,128]{2,1,0:T(8,128)(2,1)S(1)}, bf16[16,32,128]{2,1,0:T(8,128)(2,1)S(1)}, f32[32,256]{1,0:T(8,128)S(1)},...) custom-call(bf16[16,2,4096]{2,1,0:T(2,128)(2,1)} %bitcast.5, s32[16]{0:T(128)} %src_hbm.1, s32[16]{0:T(128)} %intr_hbm.1, ...), custom_call_target="tpu_custom_call" | custom-call | tf_op jit(solution)/shard_map/prepare/pallas_call | solution.py:251
  2.0 3.3 %collective-permute-start = (bf16[16,32,128]{2,1,0:T(8,128)(2,1)S(1)}, bf16[16,32,128]{2,1,0:T(8,128)(2,1)S(1)}, u32[]{:S(2)}, u32[]{:S(2)}) collective-permute-start(bf16[16,32,128]{2,1,0:T(8,128)(2,1)S(1)} %get-tuple-element.18), channel_id=1, source_target_pairs={{0,8},{8,0},{1,9},{9,1},{2,10},{10,2},{3,11},{11,3},{4,12},{12,4},... | collective-permute-start | bytes 393224 | tf_op jit(solution)/shard_map/ppermute | solution.py:282
  5.3 1.4 %lag_table.1.t_ref = bf16[8,1024,256]{2,1,0:T(8,128)(2,1)S(1)} custom-call(f32[4,64,256]{2,1,0:T(8,128)S(1)} %get-tuple-element.19.f_ref, f32[32,4096]{1,0:T(8,128)S(1)} %get-tuple-element.16._.planes_ref), custom_call_target="tpu_custom_call" | custom-call | tf_op jit(solution)/shard_map/lag_table/pallas_call | solution.py:283
  6.7 0.0 collective-permute-done
  6.8 16.1 %all_to_all.25.p_ref = bf16[16,32,128]{2,1,0:T(8,128)(2,1)S(1)} all-to-all(bf16[16,32,128]{2,1,0:T(8,128)(2,1)S(1)} %add.3), channel_id=1, replica_groups=mesh['z'=8,'xlo'=2,'core'=2,'xhi'=2,'y'=4] {'z','xlo'}, dimensions={0} | all-to-all | bytes 262144 | tf_op jit(solution)/shard_map/all_to_all | solution.py:287
  23.0 11.2 %all_to_all.26.v_ref = bf16[16,32,128]{2,1,0:T(8,128)(2,1)S(1)} all-to-all(bf16[16,32,128]{2,1,0:T(8,128)(2,1)S(1)} %spread.1), channel_id=1, replica_groups=mesh['z'=8,'xlo'=2,'core'=2,'xhi'=2,'y'=4] {'z','xlo'}, dimensions={0} | all-to-all | bytes 262144 | tf_op jit(solution)/shard_map/all_to_all | solution.py:289
  34.2 2.8 %collective-permute-start.1 = (bf16[16,32,128]{2,1,0:T(8,128)(2,1)S(1)}, bf16[16,32,128]{2,1,0:T(8,128)(2,1)S(1)}, u32[]{:S(2)}, u32[]{:S(2)}) collective-permute-start(bf16[16,32,128]{2,1,0:T(8,128)(2,1)S(1)} %all_to_all.26.v_ref), channel_id=1, source_target_pairs={{0,8},{8,0},{1,9},{9,1},{2,10},{10,2},{3,11},{11,3},{4,12},{12,4},... | collective-permute-start | bytes 393224 | tf_op jit(solution)/shard_map/ppermute | solution.py:290
  37.0 1.4 %first_half.1.first_ref = f32[256,256]{1,0:T(8,128)S(1)} custom-call(f32[32,4096]{1,0:T(8,128)S(1)} %get-tuple-element.16._.planes_ref, bf16[16,32,128]{2,1,0:T(8,128)(2,1)S(1)} %all_to_all.26.v_ref, bf16[8,1024,256]{2,1,0:T(8,128)(2,1)S(1)} %lag_table.1.t_ref), custom_call_target="tpu_custom_call" | custom-call | tf_op jit(solution)/shard_map/first_half/pallas_call | solution.py:292
  38.4 0.0 collective-permute-done.1.v_ref
  38.5 1.4 %second_half.1 = f32[8,32,256]{2,1,0:T(8,128)S(1)} custom-call(f32[32,4096]{1,0:T(8,128)S(1)} %get-tuple-element.16._.planes_ref, bf16[16,32,128]{2,1,0:T(8,128)(2,1)S(1)} %collective-permute-done.1.v_ref, bf16[8,1024,256]{2,1,0:T(8,128)(2,1)S(1)} %lag_table.1.t_ref, f32[256,256]{1,0:T(8,128)S(1)} %first_half.1.first_ref), custom_call_target="tpu_custom_call" | custom-call | tf_op jit(solution)/shard_map/second_half/pallas_call | solution.py:295
  39.9 13.7 %all_to_all.27.c_ref = f32[8,32,256]{2,1,0:T(8,128)S(1)} all-to-all(f32[8,32,256]{2,1,0:T(8,128)S(1)} %second_half.1), channel_id=1, replica_groups=mesh['z'=8,'xlo'=2,'core'=2,'xhi'=2,'y'=4] {'xhi','y'}, dimensions={0} | all-to-all | bytes 524288 | tf_op jit(solution)/shard_map/all_to_all | solution.py:298
  53.7 0.7 drift.1
  54.4 12.4 %all_to_all.28.p_ref = f32[32,8,128]{2,1,0:T(8,128)S(1)} all-to-all(f32[32,8,128]{2,1,0:T(8,128)S(1)} %bitcast.4), channel_id=1, replica_groups=mesh['z'=8,'xlo'=2,'core'=2,'xhi'=2,'y'=4] {'xhi','xlo','core','y'}, dimensions={0} | all-to-all | bytes 262144 | tf_op jit(solution)/shard_map/all_to_all | solution.py:305
  66.8 8.9 %all_to_all.29.p_ref = f32[8,1,128]{2,1,0:T(1,128)S(1)} all-to-all(f32[8,1,128]{2,1,0:T(1,128)S(1)} %near_fits.1), channel_id=1, replica_groups=mesh['z'=8,'xlo'=2,'core'=2,'xhi'=2,'y'=4] {'z'}, dimensions={0} | all-to-all | bytes 8192 | tf_op jit(solution)/shard_map/all_to_all | solution.py:307
  75.7 0.6 finish.1
  (3 shorter events, 0.1 us)
Async XLA Ops:
  2.0 4.7 %collective-permute-start = (bf16[16,32,128]{2,1,0:T(8,128)(2,1)S(1)}, bf16[16,32,128]{2,1,0:T(8,128)(2,1)S(1)}, u32[]{:S(2)}, u32[]{:S(2)}) collective-permute-start(bf16[16,32,128]{2,1,0:T(8,128)(2,1)S(1)} %get-tuple-element.18), channel_id=1, source_target_pairs={{0,8},{8,0},{1,9},{9,1},{2,10},{10,2},{3,11},{11,3},{4,12},{12,4},... | collective-permute-start | bytes 393224 | tf_op jit(solution)/shard_map/ppermute | solution.py:282
  34.2 4.3 %collective-permute-start.1 = (bf16[16,32,128]{2,1,0:T(8,128)(2,1)S(1)}, bf16[16,32,128]{2,1,0:T(8,128)(2,1)S(1)}, u32[]{:S(2)}, u32[]{:S(2)}) collective-permute-start(bf16[16,32,128]{2,1,0:T(8,128)(2,1)S(1)} %all_to_all.26.v_ref), channel_id=1, source_target_pairs={{0,8},{8,0},{1,9},{9,1},{2,10},{10,2},{3,11},{11,3},{4,12},{12,4},... | collective-permute-start | bytes 393224 | tf_op jit(solution)/shard_map/ppermute | solution.py:290

commit v3 on v2

v3 whole, which is shorter than its diff:
```python
import math

import jax
import jax.numpy as jnp
import numpy as np
from jax import lax
from jax.experimental import pallas as pl
from jax.experimental.pallas import tpu as pltpu
from jax.sharding import Mesh, PartitionSpec as P

LAGS = 256
NINT = 8
BINS = 4096
NSRC = 16
CH = 16
LANE = 128
BF = jnp.bfloat16
F32 = jnp.float32
CHUNKS = 32
CB = BINS // CHUNKS
HALF = BINS // 2
VMEM = pl.BlockSpec(memory_space=pltpu.VMEM)
SMEM = pl.BlockSpec(memory_space=pltpu.SMEM)


def chan_index():
    return (lax.axis_index("z") * 2 + lax.axis_index("xlo")) * 2 + lax.axis_index("core")


def day_index():
    return lax.axis_index("xhi") * 4 + lax.axis_index("y")


def factor_tables():
    tau = np.arange(LAGS, dtype=np.int64)[None, :] - LAGS // 2
    coarse = 64 * np.arange(64, dtype=np.int64)[:, None] * tau
    fine = np.arange(64, dtype=np.int64)[:, None] * tau
    coarse, fine = (math.pi * (f % (2 * BINS)) / BINS for f in (coarse, fine))
    scale = 1.0 / math.sqrt(BINS)
    parts = [np.cos(coarse) * scale, -np.sin(coarse) * scale, np.cos(fine), np.sin(fine)]
    return np.concatenate(parts).astype(np.float32)


def half_range(h):
    return pl.ds(pl.multiple_of(h * HALF, HALF), HALF)


def owned_pick(src_ref):
    base = chan_index() * CH
    rows = lax.broadcasted_iota(jnp.int32, (32, 32), 0)
    cols = lax.broadcasted_iota(jnp.int32, (32, 32), 1)
    want = jnp.full((32, 32), -1, jnp.int32)
    for s in range(NSRC):
        local = src_ref[s] - base
        ok = jnp.logical_and(local >= 0, local < CH)
        first = jnp.where(ok, 2 * local, -1)
        second = jnp.where(ok, 2 * local + 1, -1)
        want = jnp.where(rows == s, first, want)
        want = jnp.where(rows == 16 + s, second, want)
    return (cols == want).astype(F32).astype(BF)


def plane_pick():
    rows = lax.broadcasted_iota(jnp.int32, (32, 32), 0)
    cols = lax.broadcasted_iota(jnp.int32, (32, 32), 1)
    return (cols == 2 * (rows % CH) + rows // CH).astype(F32).astype(BF)


def put_pieces(dst, g, srcs):
    for j in range(4):
        dst[g * 4 + j] = srcs[:, j * LANE : (j + 1) * LANE]


def other_kernel(spec_hbm, src_hbm, f_hbm, other_ref, x_ref, f_ref, raw_ref, src_ref, sems):
    load_src = pltpu.make_async_copy(src_hbm, src_ref, sems.at[0])
    load_src.start()
    part = half_range(1 - lax.axis_index("core"))
    load_x = pltpu.make_async_copy(spec_hbm.at[:, :, part], raw_ref, sems.at[1])
    load_x.start()
    load_f = pltpu.make_async_copy(f_hbm, f_ref, sems.at[2])
    load_f.start()
    load_src.wait()
    pick = owned_pick(src_ref)
    load_x.wait()
    for g in range(HALF // 512):
        at = slice(g * 512, (g + 1) * 512)
        x = raw_ref[:, :, at].reshape(2 * CH, 512)
        x_ref[:, at] = x
        put_pieces(other_ref, g, jnp.dot(pick, x, preferred_element_type=F32).astype(BF))
    load_f.wait()


def mine_kernel(
    spec_hbm,
    src_hbm,
    intr_hbm,
    bounds_hbm,
    x_ref,
    f_ref,
    mine_ref,
    t_ref,
    planes_ref,
    window_ref,
    member_ref,
    raw_ref,
    src_ref,
    intr_ref,
    bounds_ref,
    sems,
):
    core = lax.axis_index("core")
    copies = [
        pltpu.make_async_copy(a, b, sems.at[i])
        for i, (a, b) in enumerate(
            (
                (spec_hbm.at[:, :, half_range(core)], raw_ref),
                (src_hbm, src_ref),
                (intr_hbm, intr_ref),
                (bounds_hbm, bounds_ref),
            )
        )
    ]
    for copy in copies:
        copy.start()
    planes = plane_pick()

    def put_planes(h, g, got):
        off = pl.multiple_of(h * HALF + g * 512, 512)
        planes_ref[:, pl.ds(off, 512)] = got

    for g in range(HALF // 512):
        x = x_ref[:, g * 512 : (g + 1) * 512]
        put_planes(1 - core, g, jnp.dot(planes, x, preferred_element_type=F32))

    def body(a, c):
        ca = f_ref[pl.ds(core * 32 + a, 1), :]
        sa = f_ref[pl.ds(64 + core * 32 + a, 1), :]
        q = a // (CB // 64)
        for i in range(0, 64, 16):
            r = pl.multiple_of((a % (CB // 64)) * 64 + i, 16)
            cb = f_ref[128 + i : 144 + i]
            sb = f_ref[192 + i : 208 + i]
            t_ref[q, pl.ds(r, 16), :] = (ca * cb + sa * sb).astype(BF)
            t_ref[q, pl.ds(CB + r, 16), :] = (sa * cb - ca * sb).astype(BF)
        return c

    lax.fori_loop(0, HALF // 64, body, 0, unroll=2)
    for copy in copies:
        copy.wait()
    owned = owned_pick(src_ref)
    for g in range(HALF // 512):
        x = raw_ref[:, :, g * 512 : (g + 1) * 512].reshape(2 * CH, 512)
        put_pieces(mine_ref, g, jnp.dot(owned, x, preferred_element_type=F32).astype(BF))
        put_planes(core, g, jnp.dot(planes, x, preferred_element_type=F32))
    day = day_index()
    lane = lax.broadcasted_iota(jnp.int32, (32, LAGS), 1)
    rowi = lax.broadcasted_iota(jnp.int32, (32, LAGS), 0)
    first = jnp.where(rowi < CH, bounds_ref[0, 2 * day], bounds_ref[0, 2 * day + 1])
    last = jnp.where(rowi < CH, bounds_ref[1, 2 * day], bounds_ref[1, 2 * day + 1])
    window_ref[...] = jnp.logical_and(lane >= first, lane < last).astype(F32)
    rows = lax.broadcasted_iota(jnp.int32, (32, LANE), 0) % CH
    cols = lax.broadcasted_iota(jnp.int32, (32, LANE), 1)
    kind = jnp.zeros((32, LANE), jnp.int32)
    for c in range(CH):
        kind = jnp.where(rows == c, intr_ref[c], kind)
    member_ref[0] = (cols == kind).astype(F32)
    member_ref[1] = (cols == kind + NINT).astype(F32)


def other_table_kernel(t_ref, _, o_ref):
    lag = lax.broadcasted_iota(jnp.int32, (2 * 8, LAGS), 1) % 4
    turn = 1.0 - 2.0 * lax.axis_index("core").astype(F32)
    even = jnp.where(lag == 0, 1.0, jnp.where(lag == 2, -1.0, 0.0)).astype(BF)
    odd = (jnp.where(lag == 1, 1.0, jnp.where(lag == 3, -1.0, 0.0)) * turn).astype(BF)

    def body(q, c):
        for r in range(0, CB, 16):
            cos = t_ref[q, r : r + 16, :]
            sin = t_ref[q, CB + r : CB + r + 16, :]
            o_ref[q, r : r + 16, :] = cos * even + sin * odd
            o_ref[q, CB + r : CB + r + 16, :] = sin * even - cos * odd
        return c

    lax.fori_loop(0, CHUNKS // 2, body, 0)


def spread_kernel(p_ref, o_ref):
    n = p_ref.shape[0]
    total = p_ref[0]
    for i in range(1, n):
        total = total + p_ref[i]
    for i in range(n):
        o_ref[i] = total


def build_cross(planes_ref, v_ref, cross_ref, g, off):
    for j in range(CB // LANE):
        lo = pl.multiple_of(off + j * LANE, LANE)
        sr = [planes_ref[8 * i : 8 * i + 8, pl.ds(lo, LANE)] for i in range(2)]
        si = [planes_ref[16 + 8 * i : 24 + 8 * i, pl.ds(lo, LANE)] for i in range(2)]
        for s in range(NSRC):
            vr = v_ref[g * (CB // LANE) + j, pl.ds(s, 8, stride=0), :]
            vi = v_ref[g * (CB // LANE) + j, pl.ds(16 + s, 8, stride=0), :]
            xr = jnp.concatenate([a * vr + b * vi for a, b in zip(sr, si)], 0)
            xi = jnp.concatenate([b * vr - a * vi for a, b in zip(sr, si)], 0)
            row = slice(s * CH, (s + 1) * CH)
            cross_ref[row, j * LANE : (j + 1) * LANE] = xr.astype(BF)
            cross_ref[row, CB + j * LANE : CB + (j + 1) * LANE] = xi.astype(BF)


def half_correlation(planes_ref, v_ref, t_ref, cross_ref, wide_ref, half):
    per_half = CHUNKS // 2
    wide_ref[...] = v_ref[...].astype(F32)
    total = None
    for g in range(per_half):
        build_cross(planes_ref, wide_ref, cross_ref, g, (half * per_half + g) * CB)
        got = jnp.dot(cross_ref[...], t_ref[g], preferred_element_type=F32)
        total = got if total is None else total + got
    return total


def first_half_kernel(planes_ref, v_ref, t_ref, o_ref, cross_ref, wide_ref):
    core = lax.axis_index("core")
    o_ref[...] = half_correlation(planes_ref, v_ref, t_ref, cross_ref, wide_ref, core)


def second_half_kernel(planes_ref, v_ref, t_ref, first_ref, o_ref, cross_ref, wide_ref):
    core = lax.axis_index("core")
    total = half_correlation(planes_ref, v_ref, t_ref, cross_ref, wide_ref, 1 - core)
    o_ref[...] = (first_ref[...] + total).reshape(o_ref.shape)


def drift_kernel(window_ref, member_ref, c_ref, ref_ref, o_ref):
    lane = lax.broadcasted_iota(jnp.int32, (32, LAGS), 1)
    window = window_ref[...] * 0.5
    ahead_w = jnp.where(lane < LAGS - 1, window, 0.0)
    behind_w = jnp.where(lane > 0, window, 0.0)
    in_num = member_ref[0]
    in_den = member_ref[1]
    total = c_ref[0]
    for d in range(1, 8):
        total = total + c_ref[d]
    ref = (total * 0.125).astype(BF)
    ref_ref[...] = ref
    ref = ref.astype(F32)
    for d in range(8):
        corr = c_ref[d]
        slope = pltpu.roll(corr, LAGS - 1, 1) * ahead_w - pltpu.roll(corr, 1, 1) * behind_w
        num = jnp.sum(slope * (corr - ref), axis=1, keepdims=True)
        den = jnp.sum(slope * slope, axis=1, keepdims=True)
        rows = num * in_num + den * in_den
        rows = (rows[0:8] + rows[8:16]) + (rows[16:24] + rows[24:32])
        for i in range(4):
            o_ref[d // 4, i, d % 4] = rows


def repeat_sum_kernel(p_ref, o_ref):
    total = jnp.sum(jnp.sum(p_ref[...], axis=0), axis=0, keepdims=True)
    for i in range(o_ref.shape[0]):
        o_ref[i] = total


def finish_kernel(p_ref, r_ref, ref_ref, o_ref):
    ref_ref[...] = r_ref[...]
    total = jnp.sum(p_ref[...], axis=0)
    o_ref[...] = total[:, :NINT] / (total[:, NINT : 2 * NINT] + 1e-06)


def call(kernel, out_shape, in_specs, name, scratch=()):
    multi = isinstance(out_shape, (list, tuple))
    return pl.pallas_call(
        kernel,
        out_shape=out_shape,
        in_specs=in_specs,
        out_specs=[VMEM] * len(out_shape) if multi else VMEM,
        scratch_shapes=list(scratch),
        compiler_params=pltpu.CompilerParams(vmem_limit_bytes=16 << 20),
        name=name,
    )


def shaped(shape, dtype):
    return jax.ShapeDtypeStruct(shape, dtype)


PAIR = [(0, 1), (1, 0)]


def per_device(spectra, source_index, interrogator, lag_bounds):
    piece = (16, 32, LANE)
    factors = factor_tables()
    hbm = pl.BlockSpec(memory_space=pltpu.HBM)

    def keep(a):
        return pltpu.with_memory_space_constraint(a, pltpu.HBM)

    spec = keep(spectra.reshape(CH, 2, BINS))
    source_index = keep(source_index)
    half_table = (CHUNKS // 2, 2 * CB, LAGS)
    raw = pltpu.VMEM((CH, 2, HALF), BF)
    other, x, factors = call(
        other_kernel,
        [shaped(piece, BF), shaped((2 * CH, HALF), BF), shaped(factors.shape, F32)],
        [hbm] * 3,
        "other",
        [raw, pltpu.SMEM((NSRC,), jnp.int32), pltpu.SemaphoreType.DMA((3,))],
    )(spec, source_index, keep(jnp.asarray(factors)))
    got = lax.ppermute(other, "core", PAIR)
    mine, table, planes, window, member = call(
        mine_kernel,
        [
            shaped(piece, BF),
            shaped(half_table, BF),
            shaped((32, BINS), F32),
            shaped((32, LAGS), F32),
            shaped((2, 32, LANE), F32),
        ],
        [hbm] * 4 + [VMEM] * 2,
        "mine",
        [
            raw,
            pltpu.SMEM((NSRC,), jnp.int32),
            pltpu.SMEM((CH,), jnp.int32),
            pltpu.SMEM((2, NSRC), jnp.int32),
            pltpu.SemaphoreType.DMA((4,)),
        ],
    )(spec, source_index, keep(interrogator), keep(lag_bounds.T), x, factors)
    parts = lax.all_to_all(mine + got, ("z", "xlo"), 0, 0)
    parts = call(spread_kernel, shaped(piece, BF), [VMEM], "spread")(parts)
    mine_half = lax.all_to_all(parts, ("z", "xlo"), 0, 0)
    other_half = lax.ppermute(mine_half, "core", PAIR)
    crosses = [pltpu.VMEM((NSRC * CH, 2 * CB), BF), pltpu.VMEM(piece, F32)]
    first = call(
        first_half_kernel, shaped((NSRC * CH, LAGS), F32), [VMEM] * 3, "first_half", crosses
    )(planes, mine_half, table)
    other_table = call(
        other_table_kernel,
        shaped(half_table, BF),
        [VMEM, pl.BlockSpec(memory_space=pl.ANY)],
        "other_table",
    )(table, first)
    other_half, other_table = lax.optimization_barrier((other_half, other_table))
    corr = call(
        second_half_kernel, shaped((8, 32, LAGS), F32), [VMEM] * 4, "second_half", crosses
    )(planes, other_half, other_table, first)
    days = lax.all_to_all(corr, ("xhi", "y"), 0, 0)
    ref, fits = call(
        drift_kernel,
        [shaped((32, LAGS), BF), shaped((2, 4, 4, 8, LANE), F32)],
        [VMEM] * 3,
        "drift",
    )(window, member, days)
    fits = lax.all_to_all(fits.reshape(32, 8, LANE), ("xhi", "xlo", "core", "y"), 0, 0)
    fits = call(repeat_sum_kernel, shaped((8, 1, LANE), F32), [VMEM], "near_fits")(fits)
    fits = lax.all_to_all(fits, "z", 0, 0)
    ref, drift = call(
        finish_kernel,
        [shaped((32, LAGS), BF), shaped((1, NINT), F32)],
        [VMEM] * 2,
        "finish",
    )(fits, ref)
    return ref.reshape(2, CH, LAGS), drift


def solution(mesh):
    fine = Mesh(mesh.devices.reshape(8, 2, 2, 2, 4), ("z", "xlo", "core", "xhi", "y"))
    chan = ("z", "xlo", "core")
    day = ("xhi", "y")
    return jax.shard_map(
        per_device,
        mesh=fine,
        in_specs=(P(day, chan, None, None), P(), P(chan), P()),
        out_specs=(P(day, chan, None), P(day, None)),
        check_vma=False,
    )
```

time: 76.6 us -> 75.1 us (0.980)
  Pallas kernels: 7.05 us -> 5.5 us
    pallas_call x2 -> x3, Pallas kernels: 2.79 us -> 2.66 us  [the longest x1 1.24 us: per_device(): call(mine_kernel, [shaped(piece, BF), shaped(half_table, BF), shaped((32,...]
  transfers between devices with their start and end apart: 2 -> 2, of which waited for: 0 -> 0; matrix products, arithmetic and copies ran while one was open for 0% -> 0% of each run, Pallas kernels for 4% -> 3%
where the time goes in v3:
time: 75.1 us; the launch traced here: 74.8 us
  blocking collectives  62.4 us (83%)
  starting transfers between devices  6.16 us (8%)
  Pallas kernels  5.5 us (7%)
    all_to_all x1, blocking collectives, per_device(): parts = lax.all_to_all(mine + got, ('z', 'xlo'), 0, 0)  16.1 us
    all_to_all x1, blocking collectives, per_device(): days = lax.all_to_all(corr, ('xhi', 'y'), 0, 0)  13.7 us
    all_to_all x1, blocking collectives, per_device(): lax.all_to_all(fits.reshape(32, 8, LANE), ('xhi', 'xlo', 'core', 'y'), 0, 0)  12.4 us
    all_to_all x1, blocking collectives, per_device(): mine_half = lax.all_to_all(parts, ('z', 'xlo'), 0, 0)  11.2 us
    all_to_all x1, blocking collectives, per_device(): fits = lax.all_to_all(fits, 'z', 0, 0)  8.92 us
    ppermute x1, starting transfers between devices, per_device(): got = lax.ppermute(other, 'core', PAIR)  3.29 us
    ppermute x1, starting transfers between devices, per_device(): other_half = lax.ppermute(mine_half, 'core', PAIR)  2.87 us
  transfers between devices with their start and end apart: 2, of which 0 were waited for; matrix products, arithmetic and copies ran while one was open for 0% of the time, Pallas kernels for 3%

profile of v3, /device:TPU:1, one launch (start us, length us, event | category | flops | bytes accessed | tf_op | source)
XLA Modules:
  0.0 74.8 jit_solution(9812176337334536618)
XLA Ops:
  0.6 1.1 %other.1 = (bf16[16,32,128]{2,1,0:T(8,128)(2,1)S(1)}, bf16[32,2048]{1,0:T(8,128)(2,1)S(1)}, f32[256,256]{1,0:T(8,128)S(1)}) custom-call(bf16[16,2,4096]{2,1,0:T(2,128)(2,1)} %bitcast.5, s32[16]{0:T(128)} %src_hbm.3, f32[256,256]{1,0:T(8,128)} %constant.2.clone.f_hbm), custom_call_target="tpu_custom_call" | custom-call | tf_op jit(solution)/shard_map/other/pallas_call | solution.py:301
  1.8 3.3 %collective-permute-start = (bf16[16,32,128]{2,1,0:T(8,128)(2,1)S(1)}, bf16[16,32,128]{2,1,0:T(8,128)(2,1)S(1)}, u32[]{:S(2)}, u32[]{:S(2)}) collective-permute-start(bf16[16,32,128]{2,1,0:T(8,128)(2,1)S(1)} %get-tuple-element.22), channel_id=1, source_target_pairs={{0,8},{8,0},{1,9},{9,1},{2,10},{10,2},{3,11},{11,3},{4,12},{12,4},... | collective-permute-start | bytes 393224 | tf_op jit(solution)/shard_map/ppermute | solution.py:308
  5.1 1.2 %mine.1 = (bf16[16,32,128]{2,1,0:T(8,128)(2,1)S(1)}, bf16[16,256,256]{2,1,0:T(8,128)(2,1)S(1)}, f32[32,4096]{1,0:T(8,128)S(1)}, f32[32,256]{1,0:T(8,128)S(1)}, f32[2,32,128]{2,1,0:T(8,128)S(1)}) custom-call(bf16[16,2,4096]{2,1,0:T(2,128)(2,1)} %bitcast.6, s32[16]{0:T(128)} %src_hbm.3, s32[16]{0:T(128)} %intr_hbm.1, s32[2,16]{1,0:T(2,128)} %bitcast.7, ...), custom_call_target="tpu_custom_call" | custom-call | tf_op jit(solution)/shard_map/mine/pallas_call | solution.py:309
  6.3 0.0 collective-permute-done
  6.4 16.1 %all_to_all.25.p_ref = bf16[16,32,128]{2,1,0:T(8,128)(2,1)S(1)} all-to-all(bf16[16,32,128]{2,1,0:T(8,128)(2,1)S(1)} %add.3), channel_id=1, replica_groups=mesh['z'=8,'xlo'=2,'core'=2,'xhi'=2,'y'=4] {'z','xlo'}, dimensions={0} | all-to-all | bytes 262144 | tf_op jit(solution)/shard_map/all_to_all | solution.py:328
  22.5 11.2 %all_to_all.26.v_ref = bf16[16,32,128]{2,1,0:T(8,128)(2,1)S(1)} all-to-all(bf16[16,32,128]{2,1,0:T(8,128)(2,1)S(1)} %spread.1), channel_id=1, replica_groups=mesh['z'=8,'xlo'=2,'core'=2,'xhi'=2,'y'=4] {'z','xlo'}, dimensions={0} | all-to-all | bytes 262144 | tf_op jit(solution)/shard_map/all_to_all | solution.py:330
  33.7 2.9 %collective-permute-start.1 = (bf16[16,32,128]{2,1,0:T(8,128)(2,1)S(1)}, bf16[16,32,128]{2,1,0:T(8,128)(2,1)S(1)}, u32[]{:S(2)}, u32[]{:S(2)}) collective-permute-start(bf16[16,32,128]{2,1,0:T(8,128)(2,1)S(1)} %all_to_all.26.v_ref), channel_id=1, source_target_pairs={{0,8},{8,0},{1,9},{9,1},{2,10},{10,2},{3,11},{11,3},{4,12},{12,4},... | collective-permute-start | bytes 393224 | tf_op jit(solution)/shard_map/ppermute | solution.py:331
  36.6 0.7 first_half.1._.first_ref
  37.3 0.3 other_table.1.t_ref
  37.6 0.0 collective-permute-done.1.v_ref
  37.6 0.7 second_half.1
  38.4 13.7 %all_to_all.27.c_ref = f32[8,32,256]{2,1,0:T(8,128)S(1)} all-to-all(f32[8,32,256]{2,1,0:T(8,128)S(1)} %second_half.1), channel_id=1, replica_groups=mesh['z'=8,'xlo'=2,'core'=2,'xhi'=2,'y'=4] {'xhi','y'}, dimensions={0} | all-to-all | bytes 524288 | tf_op jit(solution)/shard_map/all_to_all | solution.py:346
  52.1 0.7 drift.1
  52.8 12.4 %all_to_all.28.p_ref = f32[32,8,128]{2,1,0:T(8,128)S(1)} all-to-all(f32[32,8,128]{2,1,0:T(8,128)S(1)} %bitcast.4), channel_id=1, replica_groups=mesh['z'=8,'xlo'=2,'core'=2,'xhi'=2,'y'=4] {'xhi','xlo','core','y'}, dimensions={0} | all-to-all | bytes 262144 | tf_op jit(solution)/shard_map/all_to_all | solution.py:353
  65.3 8.9 %all_to_all.29.p_ref = f32[8,1,128]{2,1,0:T(1,128)S(1)} all-to-all(f32[8,1,128]{2,1,0:T(1,128)S(1)} %near_fits.1), channel_id=1, replica_groups=mesh['z'=8,'xlo'=2,'core'=2,'xhi'=2,'y'=4] {'z'}, dimensions={0} | all-to-all | bytes 8192 | tf_op jit(solution)/shard_map/all_to_all | solution.py:355
  74.2 0.6 finish.1
  (3 shorter events, 0.1 us)
Async XLA Ops:
  1.8 4.5 %collective-permute-start = (bf16[16,32,128]{2,1,0:T(8,128)(2,1)S(1)}, bf16[16,32,128]{2,1,0:T(8,128)(2,1)S(1)}, u32[]{:S(2)}, u32[]{:S(2)}) collective-permute-start(bf16[16,32,128]{2,1,0:T(8,128)(2,1)S(1)} %get-tuple-element.22), channel_id=1, source_target_pairs={{0,8},{8,0},{1,9},{9,1},{2,10},{10,2},{3,11},{11,3},{4,12},{12,4},... | collective-permute-start | bytes 393224 | tf_op jit(solution)/shard_map/ppermute | solution.py:308
  33.7 3.9 %collective-permute-start.1 = (bf16[16,32,128]{2,1,0:T(8,128)(2,1)S(1)}, bf16[16,32,128]{2,1,0:T(8,128)(2,1)S(1)}, u32[]{:S(2)}, u32[]{:S(2)}) collective-permute-start(bf16[16,32,128]{2,1,0:T(8,128)(2,1)S(1)} %all_to_all.26.v_ref), channel_id=1, source_target_pairs={{0,8},{8,0},{1,9},{9,1},{2,10},{10,2},{3,11},{11,3},{4,12},{12,4},... | collective-permute-start | bytes 393224 | tf_op jit(solution)/shard_map/ppermute | solution.py:331

commit v4 on v3

--- a/solution.py
+++ b/solution.py
@@ -325,9 +325,9 @@
             pltpu.SemaphoreType.DMA((4,)),
         ],
     )(spec, source_index, keep(interrogator), keep(lag_bounds.T), x, factors)
-    parts = lax.all_to_all(mine + got, ("z", "xlo"), 0, 0)
+    parts = lax.all_to_all(mine + got, ("xlo", "z"), 0, 0)
     parts = call(spread_kernel, shaped(piece, BF), [VMEM], "spread")(parts)
-    mine_half = lax.all_to_all(parts, ("z", "xlo"), 0, 0)
+    mine_half = lax.all_to_all(parts, ("xlo", "z"), 0, 0)
     other_half = lax.ppermute(mine_half, "core", PAIR)
     crosses = [pltpu.VMEM((NSRC * CH, 2 * CB), BF), pltpu.VMEM(piece, F32)]
     first = call(

time: 75.1 us -> 73.6 us (0.980)
  blocking collectives: 62.4 us -> 61.6 us
    all_to_all x2, blocking collectives: 27.3 us -> 26.3 us  [the longest x1 14.8 us: per_device(): parts = lax.all_to_all(mine + got, ('xlo', 'z'), 0, 0)]
where the time goes in v4:
time: 73.6 us; the launch traced here: 73.3 us
  blocking collectives  61.6 us (84%)
  Pallas kernels  5.5 us (7%)
  starting transfers between devices  5.44 us (7%)
    all_to_all x1, blocking collectives, per_device(): parts = lax.all_to_all(mine + got, ('xlo', 'z'), 0, 0)  14.8 us
    all_to_all x1, blocking collectives, per_device(): days = lax.all_to_all(corr, ('xhi', 'y'), 0, 0)  13.7 us
    all_to_all x1, blocking collectives, per_device(): lax.all_to_all(fits.reshape(32, 8, LANE), ('xhi', 'xlo', 'core', 'y'), 0, 0)  12.4 us
    all_to_all x1, blocking collectives, per_device(): mine_half = lax.all_to_all(parts, ('xlo', 'z'), 0, 0)  11.5 us
    all_to_all x1, blocking collectives, per_device(): fits = lax.all_to_all(fits, 'z', 0, 0)  9.13 us
    ppermute x1, starting transfers between devices, per_device(): got = lax.ppermute(other, 'core', PAIR)  3.29 us
    ppermute x1, starting transfers between devices, per_device(): other_half = lax.ppermute(mine_half, 'core', PAIR)  2.15 us
  transfers between devices with their start and end apart: 2, of which 0 were waited for; matrix products, arithmetic and copies ran while one was open for 0% of the time, Pallas kernels for 3%

profile of v4, /device:TPU:1, one launch (start us, length us, event | category | flops | bytes accessed | tf_op | source)
XLA Modules:
  0.0 73.3 jit_solution(17468167285837886421)
XLA Ops:
  0.6 1.1 %other.1 = (bf16[16,32,128]{2,1,0:T(8,128)(2,1)S(1)}, bf16[32,2048]{1,0:T(8,128)(2,1)S(1)}, f32[256,256]{1,0:T(8,128)S(1)}) custom-call(bf16[16,2,4096]{2,1,0:T(2,128)(2,1)} %bitcast.5, s32[16]{0:T(128)} %src_hbm.3, f32[256,256]{1,0:T(8,128)} %constant.2.clone.f_hbm), custom_call_target="tpu_custom_call" | custom-call | tf_op jit(solution)/shard_map/other/pallas_call | solution.py:301
  1.8 3.3 %collective-permute-start = (bf16[16,32,128]{2,1,0:T(8,128)(2,1)S(1)}, bf16[16,32,128]{2,1,0:T(8,128)(2,1)S(1)}, u32[]{:S(2)}, u32[]{:S(2)}) collective-permute-start(bf16[16,32,128]{2,1,0:T(8,128)(2,1)S(1)} %get-tuple-element.22), channel_id=1, source_target_pairs={{0,8},{8,0},{1,9},{9,1},{2,10},{10,2},{3,11},{11,3},{4,12},{12,4},... | collective-permute-start | bytes 393224 | tf_op jit(solution)/shard_map/ppermute | solution.py:308
  5.1 1.2 %mine.1 = (bf16[16,32,128]{2,1,0:T(8,128)(2,1)S(1)}, bf16[16,256,256]{2,1,0:T(8,128)(2,1)S(1)}, f32[32,4096]{1,0:T(8,128)S(1)}, f32[32,256]{1,0:T(8,128)S(1)}, f32[2,32,128]{2,1,0:T(8,128)S(1)}) custom-call(bf16[16,2,4096]{2,1,0:T(2,128)(2,1)} %bitcast.6, s32[16]{0:T(128)} %src_hbm.3, s32[16]{0:T(128)} %intr_hbm.1, s32[2,16]{1,0:T(2,128)} %bitcast.7, ...), custom_call_target="tpu_custom_call" | custom-call | tf_op jit(solution)/shard_map/mine/pallas_call | solution.py:309
  6.3 0.0 collective-permute-done
  6.4 14.8 %all_to_all.25.p_ref = bf16[16,32,128]{2,1,0:T(8,128)(2,1)S(1)} all-to-all(bf16[16,32,128]{2,1,0:T(8,128)(2,1)S(1)} %add.3), channel_id=1, replica_groups=mesh['z'=8,'xlo'=2,'core'=2,'xhi'=2,'y'=4] {'xlo','z'}, dimensions={0} | all-to-all | bytes 262144 | tf_op jit(solution)/shard_map/all_to_all | solution.py:328
  21.2 11.5 %all_to_all.26.v_ref = bf16[16,32,128]{2,1,0:T(8,128)(2,1)S(1)} all-to-all(bf16[16,32,128]{2,1,0:T(8,128)(2,1)S(1)} %spread.1), channel_id=1, replica_groups=mesh['z'=8,'xlo'=2,'core'=2,'xhi'=2,'y'=4] {'xlo','z'}, dimensions={0} | all-to-all | bytes 262144 | tf_op jit(solution)/shard_map/all_to_all | solution.py:330
  32.7 2.1 %collective-permute-start.1 = (bf16[16,32,128]{2,1,0:T(8,128)(2,1)S(1)}, bf16[16,32,128]{2,1,0:T(8,128)(2,1)S(1)}, u32[]{:S(2)}, u32[]{:S(2)}) collective-permute-start(bf16[16,32,128]{2,1,0:T(8,128)(2,1)S(1)} %all_to_all.26.v_ref), channel_id=1, source_target_pairs={{0,8},{8,0},{1,9},{9,1},{2,10},{10,2},{3,11},{11,3},{4,12},{12,4},... | collective-permute-start | bytes 393224 | tf_op jit(solution)/shard_map/ppermute | solution.py:331
  34.9 0.7 first_half.1._.first_ref
  35.6 0.3 other_table.1.t_ref
  35.9 0.0 collective-permute-done.1.v_ref
  35.9 0.7 second_half.1
  36.6 13.7 %all_to_all.27.c_ref = f32[8,32,256]{2,1,0:T(8,128)S(1)} all-to-all(f32[8,32,256]{2,1,0:T(8,128)S(1)} %second_half.1), channel_id=1, replica_groups=mesh['z'=8,'xlo'=2,'core'=2,'xhi'=2,'y'=4] {'xhi','y'}, dimensions={0} | all-to-all | bytes 524288 | tf_op jit(solution)/shard_map/all_to_all | solution.py:346
  50.4 0.7 drift.1
  51.1 12.4 %all_to_all.28.p_ref = f32[32,8,128]{2,1,0:T(8,128)S(1)} all-to-all(f32[32,8,128]{2,1,0:T(8,128)S(1)} %bitcast.4), channel_id=1, replica_groups=mesh['z'=8,'xlo'=2,'core'=2,'xhi'=2,'y'=4] {'xhi','xlo','core','y'}, dimensions={0} | all-to-all | bytes 262144 | tf_op jit(solution)/shard_map/all_to_all | solution.py:353
  63.5 9.1 %all_to_all.29.p_ref = f32[8,1,128]{2,1,0:T(1,128)S(1)} all-to-all(f32[8,1,128]{2,1,0:T(1,128)S(1)} %near_fits.1), channel_id=1, replica_groups=mesh['z'=8,'xlo'=2,'core'=2,'xhi'=2,'y'=4] {'z'}, dimensions={0} | all-to-all | bytes 8192 | tf_op jit(solution)/shard_map/all_to_all | solution.py:355
  72.7 0.6 finish.1
  (3 shorter events, 0.1 us)
Async XLA Ops:
  1.8 4.5 %collective-permute-start = (bf16[16,32,128]{2,1,0:T(8,128)(2,1)S(1)}, bf16[16,32,128]{2,1,0:T(8,128)(2,1)S(1)}, u32[]{:S(2)}, u32[]{:S(2)}) collective-permute-start(bf16[16,32,128]{2,1,0:T(8,128)(2,1)S(1)} %get-tuple-element.22), channel_id=1, source_target_pairs={{0,8},{8,0},{1,9},{9,1},{2,10},{10,2},{3,11},{11,3},{4,12},{12,4},... | collective-permute-start | bytes 393224 | tf_op jit(solution)/shard_map/ppermute | solution.py:308
  32.7 3.2 %collective-permute-start.1 = (bf16[16,32,128]{2,1,0:T(8,128)(2,1)S(1)}, bf16[16,32,128]{2,1,0:T(8,128)(2,1)S(1)}, u32[]{:S(2)}, u32[]{:S(2)}) collective-permute-start(bf16[16,32,128]{2,1,0:T(8,128)(2,1)S(1)} %all_to_all.26.v_ref), channel_id=1, source_target_pairs={{0,8},{8,0},{1,9},{9,1},{2,10},{10,2},{3,11},{11,3},{4,12},{12,4},... | collective-permute-start | bytes 393224 | tf_op jit(solution)/shard_map/ppermute | solution.py:331

commit v5 on v4

--- a/solution.py
+++ b/solution.py
@@ -250,8 +250,9 @@
         den = jnp.sum(slope * slope, axis=1, keepdims=True)
         rows = num * in_num + den * in_den
         rows = (rows[0:8] + rows[8:16]) + (rows[16:24] + rows[24:32])
+        row = jnp.sum(rows, axis=0, keepdims=True)
         for i in range(4):
-            o_ref[d // 4, i, d % 4] = rows
+            o_ref[d // 4, i, d % 4] = row
 
 
 def repeat_sum_kernel(p_ref, o_ref):
@@ -346,11 +347,11 @@
     days = lax.all_to_all(corr, ("xhi", "y"), 0, 0)
     ref, fits = call(
         drift_kernel,
-        [shaped((32, LAGS), BF), shaped((2, 4, 4, 8, LANE), F32)],
+        [shaped((32, LAGS), BF), shaped((2, 4, 4, 1, LANE), F32)],
         [VMEM] * 3,
         "drift",
     )(window, member, days)
-    fits = lax.all_to_all(fits.reshape(32, 8, LANE), ("xhi", "xlo", "core", "y"), 0, 0)
+    fits = lax.all_to_all(fits.reshape(32, 1, LANE), ("xhi", "xlo", "core", "y"), 0, 0)
     fits = call(repeat_sum_kernel, shaped((8, 1, LANE), F32), [VMEM], "near_fits")(fits)
     fits = lax.all_to_all(fits, "z", 0, 0)
     ref, drift = call(

time: 73.6 us -> 72.9 us (level)
  no operation moved by 1% of the time
where the time goes in v5:
time: 72.9 us; the launch traced here: 72.6 us
  blocking collectives  61 us (84%)
  Pallas kernels  5.49 us (8%)
  starting transfers between devices  5.44 us (7%)
    all_to_all x1, blocking collectives, per_device(): parts = lax.all_to_all(mine + got, ('xlo', 'z'), 0, 0)  14.8 us
    all_to_all x1, blocking collectives, per_device(): days = lax.all_to_all(corr, ('xhi', 'y'), 0, 0)  13.7 us
    all_to_all x1, blocking collectives, per_device(): lax.all_to_all(fits.reshape(32, 1, LANE), ('xhi', 'xlo', 'core', 'y'), 0, 0)  11.8 us
    all_to_all x1, blocking collectives, per_device(): mine_half = lax.all_to_all(parts, ('xlo', 'z'), 0, 0)  11.5 us
    all_to_all x1, blocking collectives, per_device(): fits = lax.all_to_all(fits, 'z', 0, 0)  9.13 us
    ppermute x1, starting transfers between devices, per_device(): got = lax.ppermute(other, 'core', PAIR)  3.29 us
    ppermute x1, starting transfers between devices, per_device(): other_half = lax.ppermute(mine_half, 'core', PAIR)  2.15 us
  transfers between devices with their start and end apart: 2, of which 0 were waited for; matrix products, arithmetic and copies ran while one was open for 0% of the time, Pallas kernels for 3%

profile of v5, /device:TPU:1, one launch (start us, length us, event | category | flops | bytes accessed | tf_op | source)
XLA Modules:
  0.0 72.6 jit_solution(9080079111079109526)
XLA Ops:
  0.6 1.1 %other.1 = (bf16[16,32,128]{2,1,0:T(8,128)(2,1)S(1)}, bf16[32,2048]{1,0:T(8,128)(2,1)S(1)}, f32[256,256]{1,0:T(8,128)S(1)}) custom-call(bf16[16,2,4096]{2,1,0:T(2,128)(2,1)} %bitcast.5, s32[16]{0:T(128)} %src_hbm.3, f32[256,256]{1,0:T(8,128)} %constant.2.clone.f_hbm), custom_call_target="tpu_custom_call" | custom-call | tf_op jit(solution)/shard_map/other/pallas_call | solution.py:302
  1.8 3.3 %collective-permute-start = (bf16[16,32,128]{2,1,0:T(8,128)(2,1)S(1)}, bf16[16,32,128]{2,1,0:T(8,128)(2,1)S(1)}, u32[]{:S(2)}, u32[]{:S(2)}) collective-permute-start(bf16[16,32,128]{2,1,0:T(8,128)(2,1)S(1)} %get-tuple-element.22), channel_id=1, source_target_pairs={{0,8},{8,0},{1,9},{9,1},{2,10},{10,2},{3,11},{11,3},{4,12},{12,4},... | collective-permute-start | bytes 393224 | tf_op jit(solution)/shard_map/ppermute | solution.py:309
  5.1 1.2 %mine.1 = (bf16[16,32,128]{2,1,0:T(8,128)(2,1)S(1)}, bf16[16,256,256]{2,1,0:T(8,128)(2,1)S(1)}, f32[32,4096]{1,0:T(8,128)S(1)}, f32[32,256]{1,0:T(8,128)S(1)}, f32[2,32,128]{2,1,0:T(8,128)S(1)}) custom-call(bf16[16,2,4096]{2,1,0:T(2,128)(2,1)} %bitcast.6, s32[16]{0:T(128)} %src_hbm.3, s32[16]{0:T(128)} %intr_hbm.1, s32[2,16]{1,0:T(2,128)} %bitcast.7, ...), custom_call_target="tpu_custom_call" | custom-call | tf_op jit(solution)/shard_map/mine/pallas_call | solution.py:310
  6.3 0.0 collective-permute-done
  6.4 14.8 %all_to_all.25.p_ref = bf16[16,32,128]{2,1,0:T(8,128)(2,1)S(1)} all-to-all(bf16[16,32,128]{2,1,0:T(8,128)(2,1)S(1)} %add.3), channel_id=1, replica_groups=mesh['z'=8,'xlo'=2,'core'=2,'xhi'=2,'y'=4] {'xlo','z'}, dimensions={0} | all-to-all | bytes 262144 | tf_op jit(solution)/shard_map/all_to_all | solution.py:329
  21.2 11.5 %all_to_all.26.v_ref = bf16[16,32,128]{2,1,0:T(8,128)(2,1)S(1)} all-to-all(bf16[16,32,128]{2,1,0:T(8,128)(2,1)S(1)} %spread.1), channel_id=1, replica_groups=mesh['z'=8,'xlo'=2,'core'=2,'xhi'=2,'y'=4] {'xlo','z'}, dimensions={0} | all-to-all | bytes 262144 | tf_op jit(solution)/shard_map/all_to_all | solution.py:331
  32.7 2.1 %collective-permute-start.1 = (bf16[16,32,128]{2,1,0:T(8,128)(2,1)S(1)}, bf16[16,32,128]{2,1,0:T(8,128)(2,1)S(1)}, u32[]{:S(2)}, u32[]{:S(2)}) collective-permute-start(bf16[16,32,128]{2,1,0:T(8,128)(2,1)S(1)} %all_to_all.26.v_ref), channel_id=1, source_target_pairs={{0,8},{8,0},{1,9},{9,1},{2,10},{10,2},{3,11},{11,3},{4,12},{12,4},... | collective-permute-start | bytes 393224 | tf_op jit(solution)/shard_map/ppermute | solution.py:332
  34.9 0.7 first_half.1._.first_ref
  35.6 0.3 other_table.1.t_ref
  35.9 0.0 collective-permute-done.1.v_ref
  35.9 0.7 %second_half.1 = f32[8,32,256]{2,1,0:T(8,128)S(1)} custom-call(f32[32,4096]{1,0:T(8,128)S(1)} %get-tuple-element.20.planes_ref, bf16[16,32,128]{2,1,0:T(8,128)(2,1)S(1)} %collective-permute-done.1.v_ref, bf16[16,256,256]{2,1,0:T(8,128)(2,1)S(1)} %other_table.1.t_ref, f32[256,256]{1,0:T(8,128)S(1)} %first_half.1._.first_ref), custom_call_target="tpu_custom_call" | custom-call | tf_op jit(solution)/shard_map/second_half/pallas_call | solution.py:344
  36.6 13.7 %all_to_all.27.c_ref = f32[8,32,256]{2,1,0:T(8,128)S(1)} all-to-all(f32[8,32,256]{2,1,0:T(8,128)S(1)} %second_half.1), channel_id=1, replica_groups=mesh['z'=8,'xlo'=2,'core'=2,'xhi'=2,'y'=4] {'xhi','y'}, dimensions={0} | all-to-all | bytes 524288 | tf_op jit(solution)/shard_map/all_to_all | solution.py:347
  50.4 0.7 drift.1
  51.1 11.8 %all_to_all.28.p_ref = f32[32,1,128]{2,1,0:T(1,128)S(1)} all-to-all(f32[32,1,128]{2,1,0:T(1,128)S(1)} %bitcast.4), channel_id=1, replica_groups=mesh['z'=8,'xlo'=2,'core'=2,'xhi'=2,'y'=4] {'xhi','xlo','core','y'}, dimensions={0} | all-to-all | bytes 32768 | tf_op jit(solution)/shard_map/all_to_all | solution.py:354
  62.9 9.1 %all_to_all.29.p_ref = f32[8,1,128]{2,1,0:T(1,128)S(1)} all-to-all(f32[8,1,128]{2,1,0:T(1,128)S(1)} %near_fits.1), channel_id=1, replica_groups=mesh['z'=8,'xlo'=2,'core'=2,'xhi'=2,'y'=4] {'z'}, dimensions={0} | all-to-all | bytes 8192 | tf_op jit(solution)/shard_map/all_to_all | solution.py:356
  72.0 0.6 finish.1
  (3 shorter events, 0.1 us)
Async XLA Ops:
  1.8 4.5 %collective-permute-start = (bf16[16,32,128]{2,1,0:T(8,128)(2,1)S(1)}, bf16[16,32,128]{2,1,0:T(8,128)(2,1)S(1)}, u32[]{:S(2)}, u32[]{:S(2)}) collective-permute-start(bf16[16,32,128]{2,1,0:T(8,128)(2,1)S(1)} %get-tuple-element.22), channel_id=1, source_target_pairs={{0,8},{8,0},{1,9},{9,1},{2,10},{10,2},{3,11},{11,3},{4,12},{12,4},... | collective-permute-start | bytes 393224 | tf_op jit(solution)/shard_map/ppermute | solution.py:309
  32.7 3.2 %collective-permute-start.1 = (bf16[16,32,128]{2,1,0:T(8,128)(2,1)S(1)}, bf16[16,32,128]{2,1,0:T(8,128)(2,1)S(1)}, u32[]{:S(2)}, u32[]{:S(2)}) collective-permute-start(bf16[16,32,128]{2,1,0:T(8,128)(2,1)S(1)} %all_to_all.26.v_ref), channel_id=1, source_target_pairs={{0,8},{8,0},{1,9},{9,1},{2,10},{10,2},{3,11},{11,3},{4,12},{12,4},... | collective-permute-start | bytes 393224 | tf_op jit(solution)/shard_map/ppermute | solution.py:332

commit v6 on v5

--- a/solution.py
+++ b/solution.py
@@ -159,12 +159,16 @@
     last = jnp.where(rowi < CH, bounds_ref[1, 2 * day], bounds_ref[1, 2 * day + 1])
     window_ref[...] = jnp.logical_and(lane >= first, lane < last).astype(F32)
     rows = lax.broadcasted_iota(jnp.int32, (32, LANE), 0) % CH
-    cols = lax.broadcasted_iota(jnp.int32, (32, LANE), 1)
-    kind = jnp.zeros((32, LANE), jnp.int32)
+    early = jnp.zeros((32, LANE), F32)
     for c in range(CH):
-        kind = jnp.where(rows == c, intr_ref[c], kind)
-    member_ref[0] = (cols == kind).astype(F32)
-    member_ref[1] = (cols == kind + NINT).astype(F32)
+        same = jnp.where(intr_ref[c] == intr_ref[0], 1.0, 0.0)
+        early = jnp.where(rows == c, same, early)
+    member_ref[0] = early
+    kind = lax.broadcasted_iota(jnp.int32, (8, LANE), 1)
+    for i, k in enumerate((intr_ref[0], intr_ref[CH - 1])):
+        for j in range(2):
+            at = slice(16 * i + 8 * j, 16 * i + 8 * j + 8)
+            member_ref[1, at] = (kind == k + NINT * j).astype(F32)
 
 
 def other_table_kernel(t_ref, _, o_ref):
@@ -235,8 +239,16 @@
     window = window_ref[...] * 0.5
     ahead_w = jnp.where(lane < LAGS - 1, window, 0.0)
     behind_w = jnp.where(lane > 0, window, 0.0)
-    in_num = member_ref[0]
-    in_den = member_ref[1]
+    early = member_ref[0]
+    lanes = [member_ref[1, 8 * i : 8 * i + 8] for i in range(4)]
+
+    def fold(x):
+        x = x[:, :LANE] + x[:, LANE:]
+        parts = []
+        for y in (x * early, x - x * early):
+            parts.append((y[0:8] + y[8:16]) + (y[16:24] + y[24:32]))
+        return [jnp.sum(y, axis=1, keepdims=True) for y in parts]
+
     total = c_ref[0]
     for d in range(1, 8):
         total = total + c_ref[d]
@@ -246,10 +258,9 @@
     for d in range(8):
         corr = c_ref[d]
         slope = pltpu.roll(corr, LAGS - 1, 1) * ahead_w - pltpu.roll(corr, 1, 1) * behind_w
-        num = jnp.sum(slope * (corr - ref), axis=1, keepdims=True)
-        den = jnp.sum(slope * slope, axis=1, keepdims=True)
-        rows = num * in_num + den * in_den
-        rows = (rows[0:8] + rows[8:16]) + (rows[16:24] + rows[24:32])
+        num = fold(slope * (corr - ref))
+        den = fold(slope * slope)
+        rows = (num[0] * lanes[0] + den[0] * lanes[1]) + (num[1] * lanes[2] + den[1] * lanes[3])
         row = jnp.sum(rows, axis=0, keepdims=True)
         for i in range(4):
             o_ref[d // 4, i, d % 4] = row

time: 72.9 us -> 72.9 us (level)
  no operation moved by 1% of the time
where the time goes in v6:
time: 72.9 us; the launch traced here: 72.6 us
  blocking collectives  61 us (84%)
  Pallas kernels  5.44 us (7%)
  starting transfers between devices  5.44 us (7%)
    all_to_all x1, blocking collectives, per_device(): parts = lax.all_to_all(mine + got, ('xlo', 'z'), 0, 0)  14.8 us
    all_to_all x1, blocking collectives, per_device(): days = lax.all_to_all(corr, ('xhi', 'y'), 0, 0)  13.7 us
    all_to_all x1, blocking collectives, per_device(): lax.all_to_all(fits.reshape(32, 1, LANE), ('xhi', 'xlo', 'core', 'y'), 0, 0)  11.8 us
    all_to_all x1, blocking collectives, per_device(): mine_half = lax.all_to_all(parts, ('xlo', 'z'), 0, 0)  11.5 us
    all_to_all x1, blocking collectives, per_device(): fits = lax.all_to_all(fits, 'z', 0, 0)  9.13 us
    ppermute x1, starting transfers between devices, per_device(): got = lax.ppermute(other, 'core', PAIR)  3.29 us
    ppermute x1, starting transfers between devices, per_device(): other_half = lax.ppermute(mine_half, 'core', PAIR)  2.15 us
  transfers between devices with their start and end apart: 2, of which 0 were waited for; matrix products, arithmetic and copies ran while one was open for 0% of the time, Pallas kernels for 3%

profile of v6, /device:TPU:1, one launch (start us, length us, event | category | flops | bytes accessed | tf_op | source)
XLA Modules:
  0.0 72.6 jit_solution(8148813927768724651)
XLA Ops:
  0.6 1.1 %other.1 = (bf16[16,32,128]{2,1,0:T(8,128)(2,1)S(1)}, bf16[32,2048]{1,0:T(8,128)(2,1)S(1)}, f32[256,256]{1,0:T(8,128)S(1)}) custom-call(bf16[16,2,4096]{2,1,0:T(2,128)(2,1)} %bitcast.5, s32[16]{0:T(128)} %src_hbm.3, f32[256,256]{1,0:T(8,128)} %constant.2.clone.f_hbm), custom_call_target="tpu_custom_call" | custom-call | tf_op jit(solution)/shard_map/other/pallas_call | solution.py:313
  1.8 3.3 %collective-permute-start = (bf16[16,32,128]{2,1,0:T(8,128)(2,1)S(1)}, bf16[16,32,128]{2,1,0:T(8,128)(2,1)S(1)}, u32[]{:S(2)}, u32[]{:S(2)}) collective-permute-start(bf16[16,32,128]{2,1,0:T(8,128)(2,1)S(1)} %get-tuple-element.22), channel_id=1, source_target_pairs={{0,8},{8,0},{1,9},{9,1},{2,10},{10,2},{3,11},{11,3},{4,12},{12,4},... | collective-permute-start | bytes 393224 | tf_op jit(solution)/shard_map/ppermute | solution.py:320
  5.1 1.2 %mine.1 = (bf16[16,32,128]{2,1,0:T(8,128)(2,1)S(1)}, bf16[16,256,256]{2,1,0:T(8,128)(2,1)S(1)}, f32[32,4096]{1,0:T(8,128)S(1)}, f32[32,256]{1,0:T(8,128)S(1)}, f32[2,32,128]{2,1,0:T(8,128)S(1)}) custom-call(bf16[16,2,4096]{2,1,0:T(2,128)(2,1)} %bitcast.6, s32[16]{0:T(128)} %src_hbm.3, s32[16]{0:T(128)} %intr_hbm.1, s32[2,16]{1,0:T(2,128)} %bitcast.7, ...), custom_call_target="tpu_custom_call" | custom-call | tf_op jit(solution)/shard_map/mine/pallas_call | solution.py:321
  6.3 0.0 collective-permute-done
  6.4 14.8 %all_to_all.25.p_ref = bf16[16,32,128]{2,1,0:T(8,128)(2,1)S(1)} all-to-all(bf16[16,32,128]{2,1,0:T(8,128)(2,1)S(1)} %add.3), channel_id=1, replica_groups=mesh['z'=8,'xlo'=2,'core'=2,'xhi'=2,'y'=4] {'xlo','z'}, dimensions={0} | all-to-all | bytes 262144 | tf_op jit(solution)/shard_map/all_to_all | solution.py:340
  21.2 11.5 %all_to_all.26.v_ref = bf16[16,32,128]{2,1,0:T(8,128)(2,1)S(1)} all-to-all(bf16[16,32,128]{2,1,0:T(8,128)(2,1)S(1)} %spread.1), channel_id=1, replica_groups=mesh['z'=8,'xlo'=2,'core'=2,'xhi'=2,'y'=4] {'xlo','z'}, dimensions={0} | all-to-all | bytes 262144 | tf_op jit(solution)/shard_map/all_to_all | solution.py:342
  32.7 2.1 %collective-permute-start.1 = (bf16[16,32,128]{2,1,0:T(8,128)(2,1)S(1)}, bf16[16,32,128]{2,1,0:T(8,128)(2,1)S(1)}, u32[]{:S(2)}, u32[]{:S(2)}) collective-permute-start(bf16[16,32,128]{2,1,0:T(8,128)(2,1)S(1)} %all_to_all.26.v_ref), channel_id=1, source_target_pairs={{0,8},{8,0},{1,9},{9,1},{2,10},{10,2},{3,11},{11,3},{4,12},{12,4},... | collective-permute-start | bytes 393224 | tf_op jit(solution)/shard_map/ppermute | solution.py:343
  34.9 0.7 first_half.1._.first_ref
  35.6 0.3 other_table.1.t_ref
  35.9 0.0 collective-permute-done.1.v_ref
  35.9 0.7 second_half.1
  36.6 13.7 %all_to_all.27.c_ref = f32[8,32,256]{2,1,0:T(8,128)S(1)} all-to-all(f32[8,32,256]{2,1,0:T(8,128)S(1)} %second_half.1), channel_id=1, replica_groups=mesh['z'=8,'xlo'=2,'core'=2,'xhi'=2,'y'=4] {'xhi','y'}, dimensions={0} | all-to-all | bytes 524288 | tf_op jit(solution)/shard_map/all_to_all | solution.py:358
  50.4 0.7 drift.1
  51.0 11.8 %all_to_all.28.p_ref = f32[32,1,128]{2,1,0:T(1,128)S(1)} all-to-all(f32[32,1,128]{2,1,0:T(1,128)S(1)} %bitcast.4), channel_id=1, replica_groups=mesh['z'=8,'xlo'=2,'core'=2,'xhi'=2,'y'=4] {'xhi','xlo','core','y'}, dimensions={0} | all-to-all | bytes 32768 | tf_op jit(solution)/shard_map/all_to_all | solution.py:365
  62.9 9.1 %all_to_all.29.p_ref = f32[8,1,128]{2,1,0:T(1,128)S(1)} all-to-all(f32[8,1,128]{2,1,0:T(1,128)S(1)} %near_fits.1), channel_id=1, replica_groups=mesh['z'=8,'xlo'=2,'core'=2,'xhi'=2,'y'=4] {'z'}, dimensions={0} | all-to-all | bytes 8192 | tf_op jit(solution)/shard_map/all_to_all | solution.py:367
  72.0 0.6 finish.1
  (3 shorter events, 0.1 us)
Async XLA Ops:
  1.8 4.5 %collective-permute-start = (bf16[16,32,128]{2,1,0:T(8,128)(2,1)S(1)}, bf16[16,32,128]{2,1,0:T(8,128)(2,1)S(1)}, u32[]{:S(2)}, u32[]{:S(2)}) collective-permute-start(bf16[16,32,128]{2,1,0:T(8,128)(2,1)S(1)} %get-tuple-element.22), channel_id=1, source_target_pairs={{0,8},{8,0},{1,9},{9,1},{2,10},{10,2},{3,11},{11,3},{4,12},{12,4},... | collective-permute-start | bytes 393224 | tf_op jit(solution)/shard_map/ppermute | solution.py:320
  32.7 3.2 %collective-permute-start.1 = (bf16[16,32,128]{2,1,0:T(8,128)(2,1)S(1)}, bf16[16,32,128]{2,1,0:T(8,128)(2,1)S(1)}, u32[]{:S(2)}, u32[]{:S(2)}) collective-permute-start(bf16[16,32,128]{2,1,0:T(8,128)(2,1)S(1)} %all_to_all.26.v_ref), channel_id=1, source_target_pairs={{0,8},{8,0},{1,9},{9,1},{2,10},{10,2},{3,11},{11,3},{4,12},{12,4},... | collective-permute-start | bytes 393224 | tf_op jit(solution)/shard_map/ppermute | solution.py:343

commit v7 on v6

--- a/solution.py
+++ b/solution.py
@@ -38,7 +38,8 @@
     coarse, fine = (math.pi * (f % (2 * BINS)) / BINS for f in (coarse, fine))
     scale = 1.0 / math.sqrt(BINS)
     parts = [np.cos(coarse) * scale, -np.sin(coarse) * scale, np.cos(fine), np.sin(fine)]
-    return np.concatenate(parts).astype(np.float32)
+    own = [p[h : h + 32] for h in (0, 32) for p in parts[:2]]
+    return np.concatenate(own + parts[2:]).astype(np.float32)
 
 
 def half_range(h):
@@ -77,8 +78,13 @@
     part = half_range(1 - lax.axis_index("core"))
     load_x = pltpu.make_async_copy(spec_hbm.at[:, :, part], raw_ref, sems.at[1])
     load_x.start()
-    load_f = pltpu.make_async_copy(f_hbm, f_ref, sems.at[2])
-    load_f.start()
+    own = pl.ds(pl.multiple_of(lax.axis_index("core") * 64, 64), 64)
+    loads_f = [
+        pltpu.make_async_copy(f_hbm.at[own], f_ref.at[0:64], sems.at[2]),
+        pltpu.make_async_copy(f_hbm.at[128:256], f_ref.at[64:192], sems.at[3]),
+    ]
+    for load in loads_f:
+        load.start()
     load_src.wait()
     pick = owned_pick(src_ref)
     load_x.wait()
@@ -87,7 +93,8 @@
         x = raw_ref[:, :, at].reshape(2 * CH, 512)
         x_ref[:, at] = x
         put_pieces(other_ref, g, jnp.dot(pick, x, preferred_element_type=F32).astype(BF))
-    load_f.wait()
+    for load in loads_f:
+        load.wait()
 
 
 def mine_kernel(
@@ -133,13 +140,13 @@
         put_planes(1 - core, g, jnp.dot(planes, x, preferred_element_type=F32))
 
     def body(a, c):
-        ca = f_ref[pl.ds(core * 32 + a, 1), :]
-        sa = f_ref[pl.ds(64 + core * 32 + a, 1), :]
+        ca = f_ref[pl.ds(a, 1), :]
+        sa = f_ref[pl.ds(32 + a, 1), :]
         q = a // (CB // 64)
         for i in range(0, 64, 16):
             r = pl.multiple_of((a % (CB // 64)) * 64 + i, 16)
-            cb = f_ref[128 + i : 144 + i]
-            sb = f_ref[192 + i : 208 + i]
+            cb = f_ref[64 + i : 80 + i]
+            sb = f_ref[128 + i : 144 + i]
             t_ref[q, pl.ds(r, 16), :] = (ca * cb + sa * sb).astype(BF)
             t_ref[q, pl.ds(CB + r, 16), :] = (sa * cb - ca * sb).astype(BF)
         return c
@@ -312,10 +319,10 @@
     raw = pltpu.VMEM((CH, 2, HALF), BF)
     other, x, factors = call(
         other_kernel,
-        [shaped(piece, BF), shaped((2 * CH, HALF), BF), shaped(factors.shape, F32)],
+        [shaped(piece, BF), shaped((2 * CH, HALF), BF), shaped((192, LAGS), F32)],
         [hbm] * 3,
         "other",
-        [raw, pltpu.SMEM((NSRC,), jnp.int32), pltpu.SemaphoreType.DMA((3,))],
+        [raw, pltpu.SMEM((NSRC,), jnp.int32), pltpu.SemaphoreType.DMA((4,))],
     )(spec, source_index, keep(jnp.asarray(factors)))
     got = lax.ppermute(other, "core", PAIR)
     mine, table, planes, window, member = call(

time: 72.9 us -> 72.9 us (level)
  no operation moved by 1% of the time
where the time goes in v7:
time: 72.9 us; the launch traced here: 72.6 us
  blocking collectives  60.9 us (84%)
  starting transfers between devices  5.46 us (7%)
  Pallas kernels  5.44 us (7%)
    all_to_all x1, blocking collectives, per_device(): parts = lax.all_to_all(mine + got, ('xlo', 'z'), 0, 0)  14.8 us
    all_to_all x1, blocking collectives, per_device(): days = lax.all_to_all(corr, ('xhi', 'y'), 0, 0)  13.7 us
    all_to_all x1, blocking collectives, per_device(): lax.all_to_all(fits.reshape(32, 1, LANE), ('xhi', 'xlo', 'core', 'y'), 0, 0)  11.8 us
    all_to_all x1, blocking collectives, per_device(): mine_half = lax.all_to_all(parts, ('xlo', 'z'), 0, 0)  11.5 us
    all_to_all x1, blocking collectives, per_device(): fits = lax.all_to_all(fits, 'z', 0, 0)  9.13 us
    ppermute x1, starting transfers between devices, per_device(): got = lax.ppermute(other, 'core', PAIR)  3.29 us
    ppermute x1, starting transfers between devices, per_device(): other_half = lax.ppermute(mine_half, 'core', PAIR)  2.17 us
  transfers between devices with their start and end apart: 2, of which 0 were waited for; matrix products, arithmetic and copies ran while one was open for 0% of the time, Pallas kernels for 3%

profile of v7, /device:TPU:1, one launch (start us, length us, event | category | flops | bytes accessed | tf_op | source)
XLA Modules:
  0.0 72.6 jit_solution(3601487981458514231)
XLA Ops:
  0.6 1.1 %other.1 = (bf16[16,32,128]{2,1,0:T(8,128)(2,1)S(1)}, bf16[32,2048]{1,0:T(8,128)(2,1)S(1)}, f32[192,256]{1,0:T(8,128)S(1)}) custom-call(bf16[16,2,4096]{2,1,0:T(2,128)(2,1)} %bitcast.5, s32[16]{0:T(128)} %src_hbm.3, f32[256,256]{1,0:T(8,128)} %constant.2.clone.f_hbm), custom_call_target="tpu_custom_call" | custom-call | tf_op jit(solution)/shard_map/other/pallas_call | solution.py:320
  1.8 3.3 %collective-permute-start = (bf16[16,32,128]{2,1,0:T(8,128)(2,1)S(1)}, bf16[16,32,128]{2,1,0:T(8,128)(2,1)S(1)}, u32[]{:S(2)}, u32[]{:S(2)}) collective-permute-start(bf16[16,32,128]{2,1,0:T(8,128)(2,1)S(1)} %get-tuple-element.22), channel_id=1, source_target_pairs={{0,8},{8,0},{1,9},{9,1},{2,10},{10,2},{3,11},{11,3},{4,12},{12,4},... | collective-permute-start | bytes 393224 | tf_op jit(solution)/shard_map/ppermute | solution.py:327
  5.1 1.2 %mine.1 = (bf16[16,32,128]{2,1,0:T(8,128)(2,1)S(1)}, bf16[16,256,256]{2,1,0:T(8,128)(2,1)S(1)}, f32[32,4096]{1,0:T(8,128)S(1)}, f32[32,256]{1,0:T(8,128)S(1)}, f32[2,32,128]{2,1,0:T(8,128)S(1)}) custom-call(bf16[16,2,4096]{2,1,0:T(2,128)(2,1)} %bitcast.6, s32[16]{0:T(128)} %src_hbm.3, s32[16]{0:T(128)} %intr_hbm.1, s32[2,16]{1,0:T(2,128)} %bitcast.7, ...), custom_call_target="tpu_custom_call" | custom-call | tf_op jit(solution)/shard_map/mine/pallas_call | solution.py:328
  6.3 0.0 collective-permute-done
  6.4 14.8 %all_to_all.25.p_ref = bf16[16,32,128]{2,1,0:T(8,128)(2,1)S(1)} all-to-all(bf16[16,32,128]{2,1,0:T(8,128)(2,1)S(1)} %add.3), channel_id=1, replica_groups=mesh['z'=8,'xlo'=2,'core'=2,'xhi'=2,'y'=4] {'xlo','z'}, dimensions={0} | all-to-all | bytes 262144 | tf_op jit(solution)/shard_map/all_to_all | solution.py:347
  21.2 11.5 %all_to_all.26.v_ref = bf16[16,32,128]{2,1,0:T(8,128)(2,1)S(1)} all-to-all(bf16[16,32,128]{2,1,0:T(8,128)(2,1)S(1)} %spread.1), channel_id=1, replica_groups=mesh['z'=8,'xlo'=2,'core'=2,'xhi'=2,'y'=4] {'xlo','z'}, dimensions={0} | all-to-all | bytes 262144 | tf_op jit(solution)/shard_map/all_to_all | solution.py:349
  32.7 2.2 %collective-permute-start.1 = (bf16[16,32,128]{2,1,0:T(8,128)(2,1)S(1)}, bf16[16,32,128]{2,1,0:T(8,128)(2,1)S(1)}, u32[]{:S(2)}, u32[]{:S(2)}) collective-permute-start(bf16[16,32,128]{2,1,0:T(8,128)(2,1)S(1)} %all_to_all.26.v_ref), channel_id=1, source_target_pairs={{0,8},{8,0},{1,9},{9,1},{2,10},{10,2},{3,11},{11,3},{4,12},{12,4},... | collective-permute-start | bytes 393224 | tf_op jit(solution)/shard_map/ppermute | solution.py:350
  34.9 0.7 first_half.1._.first_ref
  35.6 0.3 other_table.1.t_ref
  35.9 0.0 collective-permute-done.1.v_ref
  35.9 0.7 %second_half.1 = f32[8,32,256]{2,1,0:T(8,128)S(1)} custom-call(f32[32,4096]{1,0:T(8,128)S(1)} %get-tuple-element.20.planes_ref, bf16[16,32,128]{2,1,0:T(8,128)(2,1)S(1)} %collective-permute-done.1.v_ref, bf16[16,256,256]{2,1,0:T(8,128)(2,1)S(1)} %other_table.1.t_ref, f32[256,256]{1,0:T(8,128)S(1)} %first_half.1._.first_ref), custom_call_target="tpu_custom_call" | custom-call | tf_op jit(solution)/shard_map/second_half/pallas_call | solution.py:362
  36.6 13.7 %all_to_all.27.c_ref = f32[8,32,256]{2,1,0:T(8,128)S(1)} all-to-all(f32[8,32,256]{2,1,0:T(8,128)S(1)} %second_half.1), channel_id=1, replica_groups=mesh['z'=8,'xlo'=2,'core'=2,'xhi'=2,'y'=4] {'xhi','y'}, dimensions={0} | all-to-all | bytes 524288 | tf_op jit(solution)/shard_map/all_to_all | solution.py:365
  50.4 0.7 drift.1
  51.0 11.8 %all_to_all.28.p_ref = f32[32,1,128]{2,1,0:T(1,128)S(1)} all-to-all(f32[32,1,128]{2,1,0:T(1,128)S(1)} %bitcast.4), channel_id=1, replica_groups=mesh['z'=8,'xlo'=2,'core'=2,'xhi'=2,'y'=4] {'xhi','xlo','core','y'}, dimensions={0} | all-to-all | bytes 32768 | tf_op jit(solution)/shard_map/all_to_all | solution.py:372
  62.8 9.1 %all_to_all.29.p_ref = f32[8,1,128]{2,1,0:T(1,128)S(1)} all-to-all(f32[8,1,128]{2,1,0:T(1,128)S(1)} %near_fits.1), channel_id=1, replica_groups=mesh['z'=8,'xlo'=2,'core'=2,'xhi'=2,'y'=4] {'z'}, dimensions={0} | all-to-all | bytes 8192 | tf_op jit(solution)/shard_map/all_to_all | solution.py:374
  72.0 0.6 finish.1
  (3 shorter events, 0.1 us)
Async XLA Ops:
  1.8 4.5 %collective-permute-start = (bf16[16,32,128]{2,1,0:T(8,128)(2,1)S(1)}, bf16[16,32,128]{2,1,0:T(8,128)(2,1)S(1)}, u32[]{:S(2)}, u32[]{:S(2)}) collective-permute-start(bf16[16,32,128]{2,1,0:T(8,128)(2,1)S(1)} %get-tuple-element.22), channel_id=1, source_target_pairs={{0,8},{8,0},{1,9},{9,1},{2,10},{10,2},{3,11},{11,3},{4,12},{12,4},... | collective-permute-start | bytes 393224 | tf_op jit(solution)/shard_map/ppermute | solution.py:327
  32.7 3.2 %collective-permute-start.1 = (bf16[16,32,128]{2,1,0:T(8,128)(2,1)S(1)}, bf16[16,32,128]{2,1,0:T(8,128)(2,1)S(1)}, u32[]{:S(2)}, u32[]{:S(2)}) collective-permute-start(bf16[16,32,128]{2,1,0:T(8,128)(2,1)S(1)} %all_to_all.26.v_ref), channel_id=1, source_target_pairs={{0,8},{8,0},{1,9},{9,1},{2,10},{10,2},{3,11},{11,3},{4,12},{12,4},... | collective-permute-start | bytes 393224 | tf_op jit(solution)/shard_map/ppermute | solution.py:350

commit v8 on v7

--- a/solution.py
+++ b/solution.py
@@ -192,7 +192,7 @@
             o_ref[q, CB + r : CB + r + 16, :] = sin * even - cos * odd
         return c
 
-    lax.fori_loop(0, CHUNKS // 2, body, 0)
+    lax.fori_loop(0, CHUNKS // 2, body, 0, unroll=2)
 
 
 def spread_kernel(p_ref, o_ref):

time: 72.9 us -> 72.9 us (level)
  no operation moved by 1% of the time
where the time goes in v8:
time: 72.9 us; the launch traced here: 72.6 us
  blocking collectives  60.9 us (84%)
  starting transfers between devices  5.46 us (7%)
  Pallas kernels  5.41 us (7%)
    all_to_all x1, blocking collectives, per_device(): parts = lax.all_to_all(mine + got, ('xlo', 'z'), 0, 0)  14.8 us
    all_to_all x1, blocking collectives, per_device(): days = lax.all_to_all(corr, ('xhi', 'y'), 0, 0)  13.7 us
    all_to_all x1, blocking collectives, per_device(): lax.all_to_all(fits.reshape(32, 1, LANE), ('xhi', 'xlo', 'core', 'y'), 0, 0)  11.8 us
    all_to_all x1, blocking collectives, per_device(): mine_half = lax.all_to_all(parts, ('xlo', 'z'), 0, 0)  11.5 us
    all_to_all x1, blocking collectives, per_device(): fits = lax.all_to_all(fits, 'z', 0, 0)  9.13 us
    ppermute x1, starting transfers between devices, per_device(): got = lax.ppermute(other, 'core', PAIR)  3.29 us
    ppermute x1, starting transfers between devices, per_device(): other_half = lax.ppermute(mine_half, 'core', PAIR)  2.17 us
  transfers between devices with their start and end apart: 2, of which 0 were waited for; matrix products, arithmetic and copies ran while one was open for 0% of the time, Pallas kernels for 3%

profile of v8, /device:TPU:1, one launch (start us, length us, event | category | flops | bytes accessed | tf_op | source)
XLA Modules:
  0.0 72.6 jit_solution(12893226976993822510)
XLA Ops:
  0.6 1.1 %other.1 = (bf16[16,32,128]{2,1,0:T(8,128)(2,1)S(1)}, bf16[32,2048]{1,0:T(8,128)(2,1)S(1)}, f32[192,256]{1,0:T(8,128)S(1)}) custom-call(bf16[16,2,4096]{2,1,0:T(2,128)(2,1)} %bitcast.5, s32[16]{0:T(128)} %src_hbm.3, f32[256,256]{1,0:T(8,128)} %constant.2.clone.f_hbm), custom_call_target="tpu_custom_call" | custom-call | tf_op jit(solution)/shard_map/other/pallas_call | solution.py:320
  1.8 3.3 %collective-permute-start = (bf16[16,32,128]{2,1,0:T(8,128)(2,1)S(1)}, bf16[16,32,128]{2,1,0:T(8,128)(2,1)S(1)}, u32[]{:S(2)}, u32[]{:S(2)}) collective-permute-start(bf16[16,32,128]{2,1,0:T(8,128)(2,1)S(1)} %get-tuple-element.22), channel_id=1, source_target_pairs={{0,8},{8,0},{1,9},{9,1},{2,10},{10,2},{3,11},{11,3},{4,12},{12,4},... | collective-permute-start | bytes 393224 | tf_op jit(solution)/shard_map/ppermute | solution.py:327
  5.1 1.2 %mine.1 = (bf16[16,32,128]{2,1,0:T(8,128)(2,1)S(1)}, bf16[16,256,256]{2,1,0:T(8,128)(2,1)S(1)}, f32[32,4096]{1,0:T(8,128)S(1)}, f32[32,256]{1,0:T(8,128)S(1)}, f32[2,32,128]{2,1,0:T(8,128)S(1)}) custom-call(bf16[16,2,4096]{2,1,0:T(2,128)(2,1)} %bitcast.6, s32[16]{0:T(128)} %src_hbm.3, s32[16]{0:T(128)} %intr_hbm.1, s32[2,16]{1,0:T(2,128)} %bitcast.7, ...), custom_call_target="tpu_custom_call" | custom-call | tf_op jit(solution)/shard_map/mine/pallas_call | solution.py:328
  6.3 0.0 collective-permute-done
  6.4 14.8 %all_to_all.25.p_ref = bf16[16,32,128]{2,1,0:T(8,128)(2,1)S(1)} all-to-all(bf16[16,32,128]{2,1,0:T(8,128)(2,1)S(1)} %add.3), channel_id=1, replica_groups=mesh['z'=8,'xlo'=2,'core'=2,'xhi'=2,'y'=4] {'xlo','z'}, dimensions={0} | all-to-all | bytes 262144 | tf_op jit(solution)/shard_map/all_to_all | solution.py:347
  21.2 11.5 %all_to_all.26.v_ref = bf16[16,32,128]{2,1,0:T(8,128)(2,1)S(1)} all-to-all(bf16[16,32,128]{2,1,0:T(8,128)(2,1)S(1)} %spread.1), channel_id=1, replica_groups=mesh['z'=8,'xlo'=2,'core'=2,'xhi'=2,'y'=4] {'xlo','z'}, dimensions={0} | all-to-all | bytes 262144 | tf_op jit(solution)/shard_map/all_to_all | solution.py:349
  32.7 2.2 %collective-permute-start.1 = (bf16[16,32,128]{2,1,0:T(8,128)(2,1)S(1)}, bf16[16,32,128]{2,1,0:T(8,128)(2,1)S(1)}, u32[]{:S(2)}, u32[]{:S(2)}) collective-permute-start(bf16[16,32,128]{2,1,0:T(8,128)(2,1)S(1)} %all_to_all.26.v_ref), channel_id=1, source_target_pairs={{0,8},{8,0},{1,9},{9,1},{2,10},{10,2},{3,11},{11,3},{4,12},{12,4},... | collective-permute-start | bytes 393224 | tf_op jit(solution)/shard_map/ppermute | solution.py:350
  34.9 0.7 first_half.1._.first_ref
  35.6 0.3 other_table.1.t_ref
  35.9 0.0 collective-permute-done.1.v_ref
  35.9 0.7 %second_half.1 = f32[8,32,256]{2,1,0:T(8,128)S(1)} custom-call(f32[32,4096]{1,0:T(8,128)S(1)} %get-tuple-element.20.planes_ref, bf16[16,32,128]{2,1,0:T(8,128)(2,1)S(1)} %collective-permute-done.1.v_ref, bf16[16,256,256]{2,1,0:T(8,128)(2,1)S(1)} %other_table.1.t_ref, f32[256,256]{1,0:T(8,128)S(1)} %first_half.1._.first_ref), custom_call_target="tpu_custom_call" | custom-call | tf_op jit(solution)/shard_map/second_half/pallas_call | solution.py:362
  36.6 13.7 %all_to_all.27.c_ref = f32[8,32,256]{2,1,0:T(8,128)S(1)} all-to-all(f32[8,32,256]{2,1,0:T(8,128)S(1)} %second_half.1), channel_id=1, replica_groups=mesh['z'=8,'xlo'=2,'core'=2,'xhi'=2,'y'=4] {'xhi','y'}, dimensions={0} | all-to-all | bytes 524288 | tf_op jit(solution)/shard_map/all_to_all | solution.py:365
  50.3 0.7 drift.1
  51.0 11.8 %all_to_all.28.p_ref = f32[32,1,128]{2,1,0:T(1,128)S(1)} all-to-all(f32[32,1,128]{2,1,0:T(1,128)S(1)} %bitcast.4), channel_id=1, replica_groups=mesh['z'=8,'xlo'=2,'core'=2,'xhi'=2,'y'=4] {'xhi','xlo','core','y'}, dimensions={0} | all-to-all | bytes 32768 | tf_op jit(solution)/shard_map/all_to_all | solution.py:372
  62.8 9.1 %all_to_all.29.p_ref = f32[8,1,128]{2,1,0:T(1,128)S(1)} all-to-all(f32[8,1,128]{2,1,0:T(1,128)S(1)} %near_fits.1), channel_id=1, replica_groups=mesh['z'=8,'xlo'=2,'core'=2,'xhi'=2,'y'=4] {'z'}, dimensions={0} | all-to-all | bytes 8192 | tf_op jit(solution)/shard_map/all_to_all | solution.py:374
  71.9 0.6 finish.1
  (3 shorter events, 0.1 us)
Async XLA Ops:
  1.8 4.5 %collective-permute-start = (bf16[16,32,128]{2,1,0:T(8,128)(2,1)S(1)}, bf16[16,32,128]{2,1,0:T(8,128)(2,1)S(1)}, u32[]{:S(2)}, u32[]{:S(2)}) collective-permute-start(bf16[16,32,128]{2,1,0:T(8,128)(2,1)S(1)} %get-tuple-element.22), channel_id=1, source_target_pairs={{0,8},{8,0},{1,9},{9,1},{2,10},{10,2},{3,11},{11,3},{4,12},{12,4},... | collective-permute-start | bytes 393224 | tf_op jit(solution)/shard_map/ppermute | solution.py:327
  32.7 3.2 %collective-permute-start.1 = (bf16[16,32,128]{2,1,0:T(8,128)(2,1)S(1)}, bf16[16,32,128]{2,1,0:T(8,128)(2,1)S(1)}, u32[]{:S(2)}, u32[]{:S(2)}) collective-permute-start(bf16[16,32,128]{2,1,0:T(8,128)(2,1)S(1)} %all_to_all.26.v_ref), channel_id=1, source_target_pairs={{0,8},{8,0},{1,9},{9,1},{2,10},{10,2},{3,11},{11,3},{4,12},{12,4},... | collective-permute-start | bytes 393224 | tf_op jit(solution)/shard_map/ppermute | solution.py:350
